TPU v7x, 256 devices: a whole 4x4x8 slice. The times are simulated.
256 devices in a mesh: dp: 8 (over z), bin: 32 (over x, y, core).
Axes of the slice: x: 4, y: 4, z: 8, core: 2. Of those that a mesh axis runs over, the one named last changes fastest.
Arguments:
- embeddings: bfloat16 [196608, 256], P(('dp', 'bin')), may hold values from -8 to 8
- bin_ids: int32 [196608], P(('dp', 'bin')), may hold values from 0 to 31, as said below
- spreads: float32 [3], replicated, may hold values from 0.5 to 4
- projection: bfloat16 [256, 256], replicated, may hold values from -0.375 to 0.375
Outputs:
- grad_emb: bfloat16 [196608, 256], P(('dp', 'bin'))
- grad_w: float32 [256, 256], replicated
- loss: float32 [], replicated
Inputs may be any that keep to these rules, and one draw needn't show every extreme that they name: `bin_ids`: among the 768 jets of one device at most 48 share a mass bin, and on every device one bin holds exactly 48 of them.
All inputs are finite; a program needn't handle non-finite values.
Results may differ from a plain program's by a relative error of at most 0.0044.
The roundings to bfloat16 on the way count: a program that leaves them out, or rounds other values in their place, can miss the bound.
Values may be sent and summed in bfloat16 or wider, within the bound.
A program may use at most 64 MiB of HBM per device.

v0:
```python
import jax
import jax.numpy as jnp
from jax import lax
from jax.sharding import PartitionSpec as P


def from_partner(value, axis, bit):
    mask = 2**bit
    pairs = [(source, source ^ mask) for source in range(lax.axis_size(axis))]
    return lax.ppermute(value, axis, pairs)


def tile_terms(xa, mask_a, xb, mask_b, inv_bw):
    rows_a, width = xa.shape
    rows_b = xb.shape[0]
    block = 512
    count = rows_a // block
    sq_b = jnp.sum(jnp.square(xb.astype(jnp.float32)), 1)
    coef = inv_bw / width

    def step(carry, item):
        total, col_sum, back = carry
        xblk, mblk = item
        inner = lax.dot_general(
            xblk, xb, (((1,), (1,)), ((), ())), preferred_element_type=jnp.float32
        )
        sq_a = jnp.sum(jnp.square(xblk.astype(jnp.float32)), 1)
        dist = sq_a[:, None] + sq_b[None, :] - 2.0 * inner
        kern = jnp.zeros(dist.shape, jnp.float32)
        weight = jnp.zeros(dist.shape, jnp.float32)
        for index in range(coef.shape[0]):
            expo = jnp.exp(-dist * coef[index])
            kern = kern + expo
            weight = weight + coef[index] * expo
        pairs = mblk[:, None] * mask_b[None, :]
        total = total + jnp.sum(kern * pairs)
        gram = (weight * pairs).astype(jnp.bfloat16)
        gram_f = gram.astype(jnp.float32)
        part_a = xblk.astype(jnp.float32) * jnp.sum(gram_f, 1)[:, None] - jnp.dot(
            gram, xb, preferred_element_type=jnp.float32
        )
        return ((total, col_sum, back), part_a)

    init = (
        jnp.zeros((), jnp.float32),
        jnp.zeros((rows_b,), jnp.float32),
        jnp.zeros((rows_b, width), jnp.float32),
    )
    (total, col_sum, back), parts = lax.scan(
        step, init, (xa.reshape(count, block, width), mask_a.reshape(count, block))
    )
    part_a = parts.reshape(rows_a, width)
    part_b = xb.astype(jnp.float32) * col_sum[:, None] - back
    return (total, part_a, part_b)


def local(embeddings, bin_ids, spreads, projection):
    rows, width = embeddings.shape
    owners = lax.axis_size("bin")
    slots_per = 2 * rows // owners
    inv_bw = 1.0 / spreads
    feats = jnp.dot(embeddings, projection, preferred_element_type=jnp.float32).astype(jnp.bfloat16)
    onehot = (bin_ids[:, None] == jnp.arange(owners, dtype=jnp.int32)[None, :]).astype(jnp.int32)
    counts = jnp.sum(onehot, 0)
    slot = jnp.sum((jnp.cumsum(onehot, 0) - 1) * onehot, 1)
    outbox = jnp.zeros((owners, slots_per, width), jnp.bfloat16).at[bin_ids, slot].set(feats)
    inbox, arrived = (
        lax.all_to_all(outbox, "bin", split_axis=0, concat_axis=0, tiled=True),
        lax.all_to_all(counts[:, None], "bin", split_axis=0, concat_axis=0, tiled=True),
    )
    mine = inbox.reshape(owners * slots_per, width)
    slot_ids = jnp.arange(slots_per, dtype=jnp.int32)[None, :]
    live = (slot_ids < arrived).astype(jnp.float32).reshape(-1)
    own_n = jnp.maximum(jnp.sum(arrived).astype(jnp.float32), 1.0)
    bit = owners.bit_length() - 2
    partner, partner_arrived = from_partner((mine, arrived), "bin", bit)
    partner_live = (slot_ids < partner_arrived).astype(jnp.float32).reshape(-1)
    partner_n = jnp.maximum(jnp.sum(partner_arrived).astype(jnp.float32), 1.0)
    self_sum, self_part, unused = tile_terms(mine, live, mine, live, inv_bw)
    cross_sum, cross_part, spare = tile_terms(mine, live, partner, partner_live, inv_bw)
    cross_loss = -cross_sum / (own_n * partner_n)
    scale = float(rows * width)
    grad_feat = (
        scale * (-(4.0 / (own_n * own_n)) * self_part + 4.0 / (own_n * partner_n) * cross_part)
    ).astype(jnp.bfloat16)
    local_loss = self_sum / (own_n * own_n) + cross_loss
    homeward = lax.all_to_all(
        grad_feat.reshape(owners, slots_per, width), "bin", split_axis=0, concat_axis=0, tiled=True
    )
    grad_rows = homeward[bin_ids, slot]
    grad_emb = lax.dot_general(
        grad_rows, projection, (((1,), (1,)), ((), ())), preferred_element_type=jnp.float32
    ).astype(jnp.bfloat16)
    partial_w = lax.dot_general(
        embeddings, grad_rows, (((0,), (0,)), ((), ())), preferred_element_type=jnp.float32
    )
    replicas = lax.axis_size("dp")
    tokens_all = float(rows * replicas * owners)
    loss_sum = lax.psum(local_loss, ("dp", "bin"))
    weight_sum = lax.psum(partial_w, ("dp", "bin"))
    return (grad_emb, weight_sum / tokens_all, loss_sum / replicas)


def solution(mesh):
    return jax.shard_map(
        local,
        mesh=mesh,
        in_specs=(P(("dp", "bin"), None), P(("dp", "bin")), P(), P()),
        out_specs=(P(("dp", "bin"), None), P(), P()),
        check_vma=False,
    )
```

profile of v0, /device:TPU:1, one launch (start us, length us, event | category | flops | bytes accessed | tf_op | source)
XLA Modules:
  0.0 559.8 jit_solution(6354406823277336630)
XLA Ops:
  7.9 1.7 reduce-window.6
  10.0 0.9 convert_reduce_fusion.2
  11.6 8.6 %all-to-all-start = ((s32[32,1,1]{2,1,0:T(1,128)}), s32[32,1,1]{2,1,0:T(1,128)S(1)}, u32[]{:S(2)}, u32[]{:S(2)}) async-start(s32[32,1,1]{2,1,0:T(1,128)} %copy.13), calls=%async_computation | async-start | bytes 32768 | tf_op jit(solution)/shard_map/all_to_all | solution.py:69
  20.9 1.2 convolution_convert_fusion.1
  22.1 1.0 broadcast_in_dim.10
  23.0 84.1 %scatter_fusion = bf16[32,48,256]{2,1,0:T(8,128)(2,1)} fusion(bf16[32,48,256]{2,1,0:T(8,128)(2,1)} %broadcast_in_dim.10, s32[768]{0:T(1024)S(1)} %get-tuple-element.160, bf16[768,256]{1,0:T(8,128)(2,1)S(1)} %convolution_convert_fusion.1), kind=kCustom, calls=%fused_computation.1 | custom fusion | bytes 1185792 | tf_op jit(solution)/shard_map/scatter | solution.py:66
  107.1 7.5 %all-to-all-start.1 = ((bf16[32,48,256]{2,1,0:T(8,128)(2,1)}), bf16[32,48,256]{2,1,0:T(8,128)(2,1)}, u32[]{:S(2)}, u32[]{:S(2)}) async-start(bf16[32,48,256]{2,1,0:T(8,128)(2,1)} %scatter_fusion), calls=%async_computation.1 | async-start | bytes 1572864 | tf_op jit(solution)/shard_map/all_to_all | solution.py:68
  114.7 1.2 fusion.33
  116.0 3.0 collective-permute-start
  119.7 7.2 %collective-permute-done = s32[32,1]{0,1:T(1,128)S(1)} collective-permute-done((s32[32,1]{0,1:T(1,128)S(1)}, s32[32,1]{0,1:T(1,128)S(1)}, u32[]{:S(2)}, u32[]{:S(2)}) %collective-permute-start) | collective-permute-done | bytes 160 | tf_op jit(solution)/shard_map/ppermute | solution.py:10
  128.9 1.2 collective-permute-start.1
  130.2 1.4 multiply_reduce_fusion.1
  131.8 33.9 %while.26 = (s32[]{:T(128)}, f32[]{:T(128)}, f32[3,512,256]{2,1,0:T(8,128)S(1)}, bf16[3,512,256]{2,1,0:T(8,128)(2,1)}, f32[1536]{0:T(1024)S(1)}, /*index=5*/bf16...) while((s32[]{:T(128)}, f32[]{:T(128)}, ...), condition=%wide.region_11.12_spmd.clone, body=%wide.region_7.11_spmd.clone.sunk | while | flops 822609920 | bytes 6076697 | solution.py:49
  131.8 1.1 fusion.69
  133.8 7.0 %convert_reduce_fusion.5 = (f32[512]{0:T(512)S(1)}, bf16[512,1536]{1,0:T(8,128)(2,1)S(1)}, f32[]{:T(128)}) fusion(f32[1536]{0:T(1024)S(1)} %mul.351, f32[512]{0:T(512)S(1)} %bitcast.112, f32[]{:T(128)} %bitcast.97, f32[]{:T(128)} %bitcast.98, f32[]{:T(128)} %bitcast.99, bf16[1536,256]{1,0:T(8,128)(2,1)} %get-tuple-element.400, ...), kind=kOutput, calls=%fused_computation.11.clone.1 | convolution fusion | flops 419167744 | bytes 2641924 | tf_op jit(solution)/shard_map/while/body/eval_jaxpr/dot_general | solution.py:24
  140.7 1.8 fusion.70
  143.1 1.1 fusion.69
  145.1 7.0 %convert_reduce_fusion.5 = (f32[512]{0:T(512)S(1)}, bf16[512,1536]{1,0:T(8,128)(2,1)S(1)}, f32[]{:T(128)}) fusion(f32[1536]{0:T(1024)S(1)} %mul.351, f32[512]{0:T(512)S(1)} %bitcast.112, f32[]{:T(128)} %bitcast.97, f32[]{:T(128)} %bitcast.98, f32[]{:T(128)} %bitcast.99, bf16[1536,256]{1,0:T(8,128)(2,1)} %get-tuple-element.400, ...), kind=kOutput, calls=%fused_computation.11.clone.1 | convolution fusion | flops 419167744 | bytes 2641924 | tf_op jit(solution)/shard_map/while/body/eval_jaxpr/dot_general | solution.py:24
  152.0 1.8 fusion.70
  154.5 1.1 fusion.69
  156.4 7.0 %convert_reduce_fusion.5 = (f32[512]{0:T(512)S(1)}, bf16[512,1536]{1,0:T(8,128)(2,1)S(1)}, f32[]{:T(128)}) fusion(f32[1536]{0:T(1024)S(1)} %mul.351, f32[512]{0:T(512)S(1)} %bitcast.112, f32[]{:T(128)} %bitcast.97, f32[]{:T(128)} %bitcast.98, f32[]{:T(128)} %bitcast.99, bf16[1536,256]{1,0:T(8,128)(2,1)} %get-tuple-element.400, ...), kind=kOutput, calls=%fused_computation.11.clone.1 | convolution fusion | flops 419167744 | bytes 2641924 | tf_op jit(solution)/shard_map/while/body/eval_jaxpr/dot_general | solution.py:24
  163.4 1.8 fusion.70
  165.8 0.9 multiply_reduce_fusion
  166.8 42.6 %while.27 = (s32[]{:T(128)}, f32[]{:T(128)}, f32[3,512,256]{2,1,0:T(8,128)S(1)}, bf16[3,512,256]{2,1,0:T(8,128)(2,1)}, f32[1536]{0:T(1024)}, /*index=5*/bf16[153...) while((s32[]{:T(128)}, f32[]{:T(128)}, ...), condition=%wide.region_18.19_spmd.clone, body=%wide.region_14.18_spmd.clone.sunk | while | flops 822609920 | bytes 9273709 | solution.py:49
  166.8 1.7 fusion.76
  169.7 1.3 fusion.74
  171.1 0.8 mul.354
  171.9 7.0 %convert_reduce_fusion.6 = (f32[512]{0:T(512)S(1)}, bf16[512,1536]{1,0:T(8,128)(2,1)S(1)}, f32[]{:T(128)}) fusion(f32[1536]{0:T(1024)S(1)} %mul.354, f32[512]{0:T(512)} %bitcast.113, f32[]{:T(128)} %bitcast.108, f32[]{:T(128)} %bitcast.109, f32[]{:T(128)} %bitcast.110, bf16[1536,256]{1,0:T(8,128)(2,1)} %get-tuple-element.370, ...), kind=kOutput, calls=%fused_computation.34.clone.1 | convolution fusion | flops 419167744 | bytes 2643972 | tf_op jit(solution)/shard_map/while/body/eval_jaxpr/dot_general | solution.py:24
  178.8 1.5 fusion.77
  181.0 1.7 fusion.76
  183.9 1.3 fusion.74
  185.3 0.8 mul.354
  186.1 6.9 %convert_reduce_fusion.6 = (f32[512]{0:T(512)S(1)}, bf16[512,1536]{1,0:T(8,128)(2,1)S(1)}, f32[]{:T(128)}) fusion(f32[1536]{0:T(1024)S(1)} %mul.354, f32[512]{0:T(512)} %bitcast.113, f32[]{:T(128)} %bitcast.108, f32[]{:T(128)} %bitcast.109, f32[]{:T(128)} %bitcast.110, bf16[1536,256]{1,0:T(8,128)(2,1)} %get-tuple-element.370, ...), kind=kOutput, calls=%fused_computation.34.clone.1 | convolution fusion | flops 419167744 | bytes 2643972 | tf_op jit(solution)/shard_map/while/body/eval_jaxpr/dot_general | solution.py:24
  193.0 1.5 fusion.77
  195.3 1.7 fusion.76
  198.2 1.3 fusion.74
  199.5 0.8 mul.354
  200.3 6.9 %convert_reduce_fusion.6 = (f32[512]{0:T(512)S(1)}, bf16[512,1536]{1,0:T(8,128)(2,1)S(1)}, f32[]{:T(128)}) fusion(f32[1536]{0:T(1024)S(1)} %mul.354, f32[512]{0:T(512)} %bitcast.113, f32[]{:T(128)} %bitcast.108, f32[]{:T(128)} %bitcast.109, f32[]{:T(128)} %bitcast.110, bf16[1536,256]{1,0:T(8,128)(2,1)} %get-tuple-element.370, ...), kind=kOutput, calls=%fused_computation.34.clone.1 | convolution fusion | flops 419167744 | bytes 2643972 | tf_op jit(solution)/shard_map/while/body/eval_jaxpr/dot_general | solution.py:24
  207.2 1.5 fusion.77
  209.4 1.2 multiply_convert_fusion
  210.6 6.6 %all-to-all-start.2 = ((bf16[32,48,256]{2,1,0:T(8,128)(2,1)}), bf16[32,48,256]{2,1,0:T(8,128)(2,1)S(1)}, u32[]{:S(2)}, u32[]{:S(2)}) async-start(bf16[32,48,256]{2,1,0:T(8,128)(2,1)} %bitcast.111), calls=%async_computation.2 | async-start | bytes 1572864 | tf_op jit(solution)/shard_map/all_to_all | solution.py:87
  217.3 81.9 %psum.15 = f32[]{:T(128)} all-reduce(f32[]{:T(128)S(6)} %add.95), channel_id=1, replica_groups=mesh['dp'=8,'bin'=32] {'dp','bin'}, use_global_device_ids=true, to_apply=%region_20.21 | all-reduce | flops 1 | bytes 8 | tf_op jit(solution)/shard_map/psum | solution.py:99
  299.9 4.4 gather_fusion
  304.3 1.0 convolution_bitcast_fusion
  305.4 1.0 convolution_convert_fusion
  306.4 243.6 %all-reduce.2.cloned.1.call-done = f32[256,256]{0,1:T(8,128)} async-done(((f32[256,256]{0,1:T(8,128)}), f32[256,256]{0,1:T(8,128)}) %all-reduce.2.cloned.1.call-update) | async-done | bytes 262160 | tf_op jit(solution)/shard_map/psum | solution.py:100
  550.0 1.0 broadcast_multiply_fusion
  551.0 0.8 copy.15
  (65 shorter events, 10.6 us)
Async XLA Ops:
  7.2 13.7 %copy-start = (bf16[768,256]{1,0:T(8,128)(2,1)S(1)}, bf16[768,256]{1,0:T(8,128)(2,1)}, u32[]{:S(2)}) copy-start(bf16[768,256]{1,0:T(8,128)(2,1)} %param.8) | copy-start | bytes 1179652
  11.6 95.5 %all-to-all-start = ((s32[32,1,1]{2,1,0:T(1,128)}), s32[32,1,1]{2,1,0:T(1,128)S(1)}, u32[]{:S(2)}, u32[]{:S(2)}) async-start(s32[32,1,1]{2,1,0:T(1,128)} %copy.13), calls=%async_computation | async-start | bytes 32768 | tf_op jit(solution)/shard_map/all_to_all | solution.py:69
  107.1 7.5 %copy-start.7 = (f32[3]{0:T(128)S(1)}, f32[3]{0:T(128)}, u32[]{:S(2)}) copy-start(f32[3]{0:T(128)} %param.10) | copy-start | bytes 40
  107.1 21.8 %all-to-all-start.1 = ((bf16[32,48,256]{2,1,0:T(8,128)(2,1)}), bf16[32,48,256]{2,1,0:T(8,128)(2,1)}, u32[]{:S(2)}, u32[]{:S(2)}) async-start(bf16[32,48,256]{2,1,0:T(8,128)(2,1)} %scatter_fusion), calls=%async_computation.1 | async-start | bytes 1572864 | tf_op jit(solution)/shard_map/all_to_all | solution.py:68
  116.0 10.9 %collective-permute-start = (s32[32,1]{0,1:T(1,128)S(1)}, s32[32,1]{0,1:T(1,128)S(1)}, u32[]{:S(2)}, u32[]{:S(2)}) collective-permute-start(s32[32,1]{0,1:T(1,128)S(1)} %bitcast.115), channel_id=1, source_target_pairs={{0,16},{1,17},{2,18},{3,19},{4,20},{5,21},{6,22},{7,23},{8,24},{9,... | collective-permute-start | bytes 392 | tf_op jit(solution)/shard_map/ppermute | solution.py:10
  126.9 4.9 copy-start.6
  128.9 36.8 %collective-permute-start.1 = (bf16[1536,256]{1,0:T(8,128)(2,1)}, bf16[1536,256]{1,0:T(8,128)(2,1)S(1)}, u32[]{:S(2)}, u32[]{:S(2)}) collective-permute-start(bf16[1536,256]{1,0:T(8,128)(2,1)} %bitcast.4), channel_id=1, source_target_pairs={{0,16},{1,17},{2,18},{3,19},{4,20},{5,21},{6,22},{7,23},{8,24},{9,... | collective-permute-start | bytes 2359304 | tf_op jit(solution)/shard_map/ppermute | solution.py:10
  165.8 0.9 copy-start.1
  166.8 2.9 copy-start.4
  171.9 7.0 %copy-start.2 = (bf16[1536,256]{1,0:T(8,128)(2,1)S(1)}, bf16[1536,256]{1,0:T(8,128)(2,1)}, u32[]{:S(2)}) copy-start(bf16[1536,256]{1,0:T(8,128)(2,1)} %get-tuple-element.370) | copy-start | bytes 2359300 | tf_op jit(solution)/shard_map/while
  178.8 2.2 copy-start.5
  181.0 2.9 copy-start.4
  186.1 6.9 %copy-start.2 = (bf16[1536,256]{1,0:T(8,128)(2,1)S(1)}, bf16[1536,256]{1,0:T(8,128)(2,1)}, u32[]{:S(2)}) copy-start(bf16[1536,256]{1,0:T(8,128)(2,1)} %get-tuple-element.370) | copy-start | bytes 2359300 | tf_op jit(solution)/shard_map/while
  193.0 2.2 copy-start.5
  195.2 2.9 copy-start.4
  200.3 6.9 %copy-start.2 = (bf16[1536,256]{1,0:T(8,128)(2,1)S(1)}, bf16[1536,256]{1,0:T(8,128)(2,1)}, u32[]{:S(2)}) copy-start(bf16[1536,256]{1,0:T(8,128)(2,1)} %get-tuple-element.370) | copy-start | bytes 2359300 | tf_op jit(solution)/shard_map/while
  207.2 2.2 copy-start.5
  210.6 89.3 %all-to-all-start.2 = ((bf16[32,48,256]{2,1,0:T(8,128)(2,1)}), bf16[32,48,256]{2,1,0:T(8,128)(2,1)S(1)}, u32[]{:S(2)}, u32[]{:S(2)}) async-start(bf16[32,48,256]{2,1,0:T(8,128)(2,1)} %bitcast.111), calls=%async_computation.2 | async-start | bytes 1572864 | tf_op jit(solution)/shard_map/all_to_all | solution.py:87
  217.2 332.8 %all-reduce.2.cloned.1.call-start = ((), (), s32[]{:S(2)}) async-start(), calls=%async_computation.3 | async-start | bytes 524288 | tf_op jit(solution)/shard_map/psum | solution.py:100
  299.9 5.5 copy-start.3
Sparse Core Ops, SparseCore 0:
  305.5 244.5 all-reduce.1
where the time goes:
time: 564 us; the launch traced here: 560 us
  waiting for transfers between devices  252 us (45%)
  local copies, waits for them, and re-layouts  100 us (18%)
  blocking collectives  81.9 us (15%)
  matrix products  54.8 us (10%)
  starting transfers between devices  26.9 us (5%)
  other arithmetic  23.1 us (4%)
  between operations  17.5 us (3%)
    psum x1, waiting for transfers between devices, local(): weight_sum = lax.psum(partial_w, ('dp', 'bin'))  244 us
    scatter x1, local copies, waits for them, and re-layouts, local(): jnp.zeros((owners, slots_per, width), jnp.bfloat16).at[bin_ids, slot]  84.1 us
    psum x1, blocking collectives, local(): loss_sum = lax.psum(local_loss, ('dp', 'bin'))  81.9 us
    dot_general x6, matrix products, step(): lax.dot_general(xblk, xb, (((1,), (1,)), ((), ())), preferred_element_typ...  41.7 us
  transfers between devices with their start and end apart: 6, of which 3 were waited for; matrix products, arithmetic and copies ran while one was open for 22% of the time, Pallas kernels for 0%

commit v1 on v0

v1 whole, which is shorter than its diff:
```python
import functools
import math

import jax
import jax.numpy as jnp
from jax import lax
from jax.experimental import pallas as pl
from jax.experimental.pallas import tpu as pltpu
from jax.sharding import PartitionSpec as P

MESH = pl.DeviceIdType.MESH
F32 = jnp.float32
BF16 = jnp.bfloat16
FAR = 1e30
NT = (((1,), (1,)), ((), ()))
TN = (((0,), (0,)), ((), ()))


def iota(shape, dim):
    return lax.broadcasted_iota(jnp.int32, shape, dim)


def slot_places(ids, me, bins, cap):
    half = bins // 2
    jets = ids.shape[1]
    owner = jnp.where(ids >= half, 2 * (ids - half) + 1, 2 * ids)
    step = 256 if jets % 256 == 0 else jets
    before = jnp.where(iota((step, step), 0) < iota((step, step), 1), 1.0, 0.0).astype(BF16)
    wide = max(bins, 16)
    carry = jnp.zeros((wide, 1), F32)
    ranks = []
    for start in range(0, jets, step):
        hot = jnp.where(owner[:, start:start + step] == iota((wide, step), 0), 1.0, 0.0)
        seen = jnp.dot(hot.astype(BF16), before, preferred_element_type=F32) + carry
        ranks.append(jnp.sum(seen * hot, 0, keepdims=True))
        carry = carry + jnp.sum(hot, 1, keepdims=True)
    rank = jnp.concatenate(ranks, 1).astype(jnp.int32)
    away = owner - me
    away = jnp.where(away < 0, away + bins, away)
    return owner, away * cap + rank


def scatter_kernel(bins, cap, emb_ref, ids_ref, inbox, pinbox, counts, outbox, mine,
                   cnt_send, cnt_recv, send, recv, fwd_send, fwd_recv, loc):
    z, me = lax.axis_index("dp"), lax.axis_index("bin")
    sib = me + 1 - 2 * lax.rem(me, 2)
    jets = emb_ref.shape[0]
    barrier = pltpu.get_barrier_semaphore()
    for k in range(1, bins):
        pl.semaphore_signal(barrier, inc=1, device_id=(z, lax.rem(me + k, bins)), device_id_type=MESH)
    owner, place = slot_places(ids_ref[...], me, bins, cap)
    hot = jnp.where(owner == iota((128, jets), 0), 1.0, 0.0).astype(BF16)
    tally = lax.dot_general(jnp.ones((8, jets), BF16), hot, NT, preferred_element_type=F32)
    mine[...] = tally[0:1, :].astype(jnp.int32)
    counts[me] = tally[0:1, :].astype(jnp.int32)
    pl.semaphore_wait(barrier, bins - 1)

    def count_copy(k):
        return pltpu.make_async_remote_copy(
            src_ref=mine, dst_ref=counts.at[me], send_sem=cnt_send.at[k], recv_sem=cnt_recv.at[k],
            device_id=(z, lax.rem(me + k, bins)), device_id_type=MESH)

    def row_copy(k):
        return pltpu.make_async_remote_copy(
            src_ref=outbox.at[k], dst_ref=inbox.at[me], send_sem=send.at[k], recv_sem=recv.at[k],
            device_id=(z, lax.rem(me + k, bins)), device_id_type=MESH)

    for k in range(1, bins):
        count_copy(k).start()
    group = 8 if bins % 8 == 0 else bins
    emb = emb_ref[...]
    for first in range(0, bins, group):
        rows = group * cap
        pick = jnp.where(iota((rows, jets), 0) + first * cap == place, 1.0, 0.0).astype(BF16)
        block = jnp.dot(pick, emb, preferred_element_type=F32).astype(BF16)
        outbox[first:first + group] = block.reshape(group, cap, block.shape[1])
        for k in range(first, first + group):
            if k:
                row_copy(k).start()
    own = pltpu.make_async_copy(outbox.at[0], inbox.at[me], loc)
    own.start()

    def forward(src):
        return pltpu.make_async_remote_copy(
            src_ref=inbox.at[src], dst_ref=pinbox.at[src], send_sem=fwd_send, recv_sem=fwd_recv,
            device_id=(z, sib), device_id_type=MESH)

    own.wait()
    forward(me).start()
    for k in range(1, bins):
        row_copy(k).wait_recv()
        forward(lax.rem(me + bins - k, bins)).start()
    for k in range(1, bins):
        count_copy(k).wait()
        row_copy(k).wait_send()
    pltpu.make_async_remote_copy(
        src_ref=inbox, dst_ref=pinbox, send_sem=fwd_send, recv_sem=fwd_recv,
        device_id=(z, sib), device_id_type=MESH).wait()


def pair_kernel(bins, cap, br, bc, cnt_ref, spread_ref, proj_ref, mine_ref, other_ref, out_ref, w_ref,
                xs, ys, gs, fx, fy, sax, srx, sry, acc, rsum, tot):
    me = lax.axis_index("bin")
    width = proj_ref.shape[0]
    hw = width // 2
    sib = me + 1 - 2 * lax.rem(me, 2)

    def pack(src_ref, dst, column):
        off = 0
        for s in range(bins):
            rows = src_ref[s].astype(F32)
            dst[0, pl.ds(off, cap), :] = rows[:, :hw]
            dst[1, pl.ds(off, cap), :] = rows[:, hw:]
            off = off + cnt_ref[s, 0, column]
        dst[0, pl.ds(off, bc), :] = jnp.zeros((bc, hw), F32)
        dst[1, pl.ds(off, bc), :] = jnp.zeros((bc, hw), F32)
        return off

    n_own = pack(mine_ref, xs, me)
    n_oth = pack(other_ref, ys, sib)
    proj = proj_ref[...]
    ones = jnp.ones((8, width), BF16)

    def features(rows_ref, feat, col_sq, row_sq, n):
        def body(i, carry):
            base = pl.multiple_of(i * bc, bc)
            emb = jnp.concatenate([rows_ref[0, pl.ds(base, bc), :], rows_ref[1, pl.ds(base, bc), :]], 1).astype(BF16)
            val = jnp.dot(emb, proj, preferred_element_type=F32).astype(BF16)
            feat[pl.ds(base, bc), :] = val
            sq = jnp.square(val.astype(F32))
            high = sq.astype(BF16)
            low = (sq - high.astype(F32)).astype(BF16)
            line = lax.dot_general(ones, high, NT, preferred_element_type=F32)
            line = line + lax.dot_general(ones, low, NT, preferred_element_type=F32)
            row_sq[i] = jnp.where(iota((8, bc), 1) + base < n, line, FAR)
            if col_sq is not None:
                col = jnp.broadcast_to(jnp.sum(sq, 1, keepdims=True), (bc, 128))
                col_sq[pl.ds(base, bc), :] = jnp.where(iota((bc, 128), 0) + base < n, col, FAR)
            return carry
        blocks = (n + bc - 1) // bc
        lax.fori_loop(0, blocks, body, 0)
        return blocks

    cols_own = features(xs, fx, sax, srx, n_own)
    cols_oth = features(ys, fy, None, sry, n_oth)

    coef = [1.0 / jnp.full((1, bc), spread_ref[s], F32) / width for s in range(3)]
    rate = [c * math.log2(math.e) for c in coef]
    na = jnp.full((1, 128), jnp.maximum(n_own, 1).astype(F32), F32)
    nc = jnp.full((1, 128), jnp.maximum(n_oth, 1).astype(F32), F32)
    scale = float(bins * cap // 2 * width)
    k_self = scale * (-(4.0 / (na * na)))
    k_cross = scale * (4.0 / (na * nc))
    k_self = jnp.concatenate([k_self] * (width // 128), 1)
    k_cross = jnp.concatenate([k_cross] * (width // 128), 1)

    tot[...] = jnp.zeros_like(tot)
    w_ref[...] = jnp.zeros_like(w_ref)
    solid = jnp.ones((bc, 128), BF16)

    def row_block(i, carry):
        base = pl.multiple_of(i * br, br)
        xa = fx[pl.ds(base, br), :]
        xa2 = xa + xa
        sa = sax[pl.ds(base, br), :]
        sa = jnp.concatenate([sa] * (bc // 128), 1)

        def gather(which, feat, row_sq, blocks):
            acc[which] = jnp.zeros((br, width), F32)
            rsum[which] = jnp.zeros((br, 128), F32)

            def body(j, inner_carry):
                xb = feat[pl.ds(pl.multiple_of(j * bc, bc), bc), :]
                inner = lax.dot_general(xa2, xb, NT, preferred_element_type=F32)
                sb = row_sq[j]
                t = inner - sa - sb[0:1, :]
                e0 = jnp.exp2(t * rate[0])
                e1 = jnp.exp2(t * rate[1])
                e2 = jnp.exp2(t * rate[2])
                kern = e0 + e1 + e2
                tot[which] += jnp.sum(kern.reshape(br // 8, 8, bc), 0)
                gram = (e0 * coef[0] + e1 * coef[1] + e2 * coef[2]).astype(BF16)
                acc[which] += jnp.dot(gram, xb, preferred_element_type=F32)
                rsum[which] += jnp.dot(gram, solid, preferred_element_type=F32)
                return inner_carry
            lax.fori_loop(0, blocks, body, 0)
            total = jnp.concatenate([rsum[which]] * (width // 128), 1)
            return xa.astype(F32) * total - acc[which]

        p_self = gather(0, fx, srx, cols_own)
        p_cross = gather(1, fy, sry, cols_oth)
        gz = (k_self * p_self + k_cross * p_cross).astype(BF16)
        ge = lax.dot_general(gz, proj, NT, preferred_element_type=F32)
        gs[0, pl.ds(base, br), :] = ge[:, :hw]
        gs[1, pl.ds(base, br), :] = ge[:, hw:]
        emb = jnp.concatenate([xs[0, pl.ds(base, br), :], xs[1, pl.ds(base, br), :]], 1).astype(BF16)
        gw = lax.dot_general(emb, gz, TN, preferred_element_type=F32)
        w_ref[0, :width, :] += gw[:, :hw]
        w_ref[1, :width, :] += gw[:, hw:]
        return carry

    lax.fori_loop(0, (n_own + br - 1) // br, row_block, 0)
    gs[0, pl.ds(n_own, cap), :] = jnp.zeros((cap, hw), F32)
    gs[1, pl.ds(n_own, cap), :] = jnp.zeros((cap, hw), F32)
    line = jnp.sum(tot[0], 0, keepdims=True)[:, :128] if bc == 128 else sum(
        jnp.sum(tot[0], 0, keepdims=True)[:, p:p + 128] for p in range(0, bc, 128))
    cross = jnp.sum(tot[1], 0, keepdims=True)[:, :128] if bc == 128 else sum(
        jnp.sum(tot[1], 0, keepdims=True)[:, p:p + 128] for p in range(0, bc, 128))
    share = line / (na * na) - cross / (na * nc)
    for h in range(2):
        w_ref[h, width:width + 8, :] = jnp.broadcast_to(share, (8, 128))
    off = 0
    for s in range(bins):
        out_ref[s, :, :hw] = gs[0, pl.ds(off, cap), :].astype(BF16)
        out_ref[s, :, hw:] = gs[1, pl.ds(off, cap), :].astype(BF16)
        off = off + cnt_ref[s, 0, me]


def return_kernel(bins, reps, cap, slots, w_ref, ids_ref, g_out, w_out, l_out,
                  inbox, pick, p_recv, z_send, z_recv, a_send, a_recv, g_buf, zg, other,
                  send, recv, psem, zsem, asem, gsem, zgsem, fsem, loc):
    z, me = lax.axis_index("dp"), lax.axis_index("bin")
    core = lax.rem(me, 2)
    q = lax.div(me, 2)
    chips = bins // 2
    sib = me + 1 - 2 * core
    jets = g_out.shape[0]
    width = g_out.shape[1]
    zr = width // reps
    ar = zr // chips
    barrier = pltpu.get_barrier_semaphore()
    for k in range(1, bins):
        pl.semaphore_signal(barrier, inc=1, device_id=(z, lax.rem(me + k, bins)), device_id_type=MESH)
    for k in range(1, reps):
        pl.semaphore_signal(barrier, inc=1, device_id=(lax.rem(z + k, reps), me), device_id_type=MESH)
    pl.semaphore_wait(barrier, bins - 1 + reps - 1)

    def remote(src, dst, ssem, rsem, dev):
        return pltpu.make_async_remote_copy(
            src_ref=src, dst_ref=dst, send_sem=ssem, recv_sem=rsem, device_id=dev, device_id_type=MESH)

    pair = remote(w_ref.at[1 - core], p_recv, psem.at[0], psem.at[1], (z, sib))
    pair.start()

    def row_copy(k):
        dest = lax.rem(me + k, bins)
        return remote(slots.at[dest], inbox.at[bins - k], send, recv, (z, dest))

    for k in range(1, bins):
        row_copy(k).start()
    own = pltpu.make_async_copy(slots.at[me], inbox.at[0], loc)
    own.start()

    _, place = slot_places(ids_ref[...], me, bins, cap)
    for first in range(0, jets, 128 if jets % 128 == 0 else jets):
        size = min(128, jets - first)
        part = jnp.broadcast_to(place[:, first:first + size], (size, size))
        column = jnp.sum(jnp.where(iota((size, size), 0) == iota((size, size), 1), part, 0), 1, keepdims=True)
        pick[first:first + size, :] = jnp.where(column == iota((size, bins * cap), 1), 1.0, 0.0).astype(BF16)

    pair.wait()
    half = w_ref[core] + p_recv[...]
    loss_tile = half[width:width + 8, :]
    for k in range(reps):
        z_send[k, 0:zr, :] = half[k * zr:(k + 1) * zr, :]
        z_send[k, zr:zr + 8, :] = loss_tile

    def z_copy(k):
        dest = lax.rem(z + k, reps)
        return remote(z_send.at[dest], z_recv.at[z], zsem.at[0, k], zsem.at[1, k], (dest, me))

    for k in range(1, reps):
        z_copy(k).start()
    z_recv[z] = z_send[z]
    for k in range(1, reps):
        z_copy(k).wait()
    chunk = z_recv[0]
    for k in range(1, reps):
        chunk = chunk + z_recv[k]
    for k in range(chips):
        a_send[k, 0:ar, :] = chunk[k * ar:(k + 1) * ar, :]
        a_send[k, ar:ar + 1, :] = chunk[zr:zr + 1, :]

    def a_copy(k):
        dest = lax.rem(q + k, chips)
        return remote(a_send.at[dest], a_recv.at[q], asem.at[0, k], asem.at[1, k], (z, 2 * dest + core))

    for k in range(1, chips):
        a_copy(k).start()
    a_recv[q] = a_send[q]
    for k in range(1, chips):
        a_copy(k).wait()
    piece = a_recv[0, 0:ar + 1, :]
    for k in range(1, chips):
        piece = piece + a_recv[k, 0:ar + 1, :]
    l_out[...] = jnp.broadcast_to(jnp.sum(piece[ar:ar + 1, :], 1, keepdims=True) / reps, (1, 128))
    g_buf[q] = piece[0:ar, :]

    def g_copy(k):
        dest = lax.rem(q + k, chips)
        return remote(g_buf.at[q], g_buf.at[q], gsem.at[0, k], gsem.at[1, k], (z, 2 * dest + core))

    for k in range(1, chips):
        g_copy(k).start()
    for k in range(1, chips):
        g_copy(k).wait()
    for k in range(chips):
        zg[z, k * ar:(k + 1) * ar, :] = g_buf[k]

    def zg_copy(k):
        dest = lax.rem(z + k, reps)
        return remote(zg.at[z], zg.at[z], zgsem.at[0, k], zgsem.at[1, k], (dest, me))

    for k in range(1, reps):
        zg_copy(k).start()

    own.wait()
    remote(slots.at[pl.ds(0, bins - 1)], inbox.at[pl.ds(1, bins - 1)], send, recv, (z, sib)).wait()
    g_out[...] = jnp.dot(pick[...], inbox[...].reshape(bins * cap, width), preferred_element_type=F32).astype(BF16)

    for k in range(1, reps):
        zg_copy(k).wait()
    last = remote(zg, other, fsem.at[0], fsem.at[1], (z, sib))
    last.start()
    last.wait()
    tokens = float(jets * bins * reps)
    here = zg[...].reshape(width, 128) / tokens
    there = other[...].reshape(width, 128) / tokens
    w_out[:, 0:128] = jnp.where(core == 0, here, there)
    w_out[:, 128:256] = jnp.where(core == 0, there, here)


def vmem(count):
    return [pl.BlockSpec(memory_space=pltpu.VMEM)] * count


def local(embeddings, bin_ids, spreads, projection):
    jets, width = embeddings.shape
    bins, reps = lax.axis_size("bin"), lax.axis_size("dp")
    cap = 2 * jets // bins
    most = bins * cap
    chips = bins // 2
    ids = bin_ids.reshape(1, jets)
    dma = pltpu.SemaphoreType.DMA
    box = jax.ShapeDtypeStruct((bins, cap, width), BF16)
    limit = 48 << 20
    inbox, pinbox, counts = pl.pallas_call(
        functools.partial(scatter_kernel, bins, cap),
        out_shape=(box, box, jax.ShapeDtypeStruct((bins, 1, 128), jnp.int32)),
        in_specs=vmem(2), out_specs=tuple(vmem(3)),
        scratch_shapes=[
            pltpu.VMEM((bins, cap, width), BF16), pltpu.VMEM((1, 128), jnp.int32),
            dma((bins,)), dma((bins,)), dma((bins,)), dma((bins,)), dma, dma, dma],
        compiler_params=pltpu.CompilerParams(collective_id=0, has_side_effects=True, vmem_limit_bytes=limit),
        name="scatter",
    )(embeddings, ids)

    br, bc = 256, 256
    top = -(-most // bc) * bc
    room = top + bc
    slots, w_part = pl.pallas_call(
        functools.partial(pair_kernel, bins, cap, br, bc),
        out_shape=(box, jax.ShapeDtypeStruct((2, width + 8, 128), F32)),
        in_specs=[pl.BlockSpec(memory_space=pltpu.SMEM)] * 2 + vmem(3), out_specs=tuple(vmem(2)),
        scratch_shapes=[
            pltpu.VMEM((2, room, width // 2), F32), pltpu.VMEM((2, room, width // 2), F32),
            pltpu.VMEM((2, room, width // 2), F32),
            pltpu.VMEM((top, width), BF16), pltpu.VMEM((top, width), BF16),
            pltpu.VMEM((top, 128), F32), pltpu.VMEM((top // bc, 8, bc), F32), pltpu.VMEM((top // bc, 8, bc), F32),
            pltpu.VMEM((2, br, width), F32), pltpu.VMEM((2, br, 128), F32), pltpu.VMEM((2, 8, bc), F32)],
        compiler_params=pltpu.CompilerParams(vmem_limit_bytes=limit),
        name="pairs",
    )(counts, spreads, projection, inbox, pinbox)

    zr = width // reps
    ar = zr // chips
    ap = 4 if ar < 4 else ar + 8
    grad_emb, grad_w, loss = pl.pallas_call(
        functools.partial(return_kernel, bins, reps, cap),
        out_shape=(jax.ShapeDtypeStruct((jets, width), BF16), jax.ShapeDtypeStruct((width, width), F32),
                   jax.ShapeDtypeStruct((1, 128), F32)),
        in_specs=vmem(3), out_specs=tuple(vmem(3)),
        scratch_shapes=[
            pltpu.VMEM((bins, cap, width), BF16), pltpu.VMEM((jets, most), BF16),
            pltpu.VMEM((width + 8, 128), F32),
            pltpu.VMEM((reps, zr + 8, 128), F32), pltpu.VMEM((reps, zr + 8, 128), F32),
            pltpu.VMEM((chips, ap, 128), F32), pltpu.VMEM((chips, ap, 128), F32),
            pltpu.VMEM((chips, ar, 128), F32), pltpu.VMEM((reps, zr, 128), F32), pltpu.VMEM((reps, zr, 128), F32),
            dma, dma, dma((2,)), dma((2, reps)), dma((2, chips)), dma((2, chips)), dma((2, reps)), dma((2,)), dma],
        compiler_params=pltpu.CompilerParams(collective_id=1, has_side_effects=True, vmem_limit_bytes=limit),
        name="giveback",
    )(slots, w_part, ids)
    return grad_emb, grad_w, loss[0, 0]


def solution(mesh):
    return jax.shard_map(
        local,
        mesh=mesh,
        in_specs=(P(("dp", "bin"), None), P(("dp", "bin")), P(), P()),
        out_specs=(P(("dp", "bin"), None), P(), P()),
        check_vma=False,
    )
```

time: 564 us -> 84.8 us (0.15)
  waiting for transfers between devices: 252 us -> 0 us
  local copies, waits for them, and re-layouts: 100 us -> 3.78 us
  blocking collectives: 81.9 us -> 0 us
  Pallas kernels: 0 us -> 79 us
  matrix products: 54.8 us -> 0 us
  starting transfers between devices: 26.9 us -> 0 us
  other arithmetic: 23.1 us -> 0 us
  between operations: 17.5 us -> 1.84 us
    psum x1 -> x0, waiting for transfers between devices: 244 us -> none  [local(): weight_sum = lax.psum(partial_w, ('dp', 'bin'))]
    scatter x1 -> x0, local copies, waits for them, and re-layouts: 84.1 us -> none  [local(): jnp.zeros((owners, slots_per, width), jnp.bfloat16).at[bin_ids, slot]]
    psum x1 -> x0, blocking collectives: 81.9 us -> none  [local(): loss_sum = lax.psum(local_loss, ('dp', 'bin'))]
    pallas_call x0 -> x3, Pallas kernels: none -> 79 us  [the longest x1 35.6 us: local(): pl.pallas_call(functools.partial(return_kernel, bins, reps, cap), out_sha...]
    dot_general x15 -> x0, matrix products: 54.8 us -> none  [the longest x6 41.7 us: step(): lax.dot_general(xblk, xb, (((1,), (1,)), ((), ())), preferred_element_typ...]
    all_to_all x3 -> x0, starting transfers between devices: 22.7 us -> none  [the longest x1 8.59 us: local(): lax.all_to_all(counts[:, None], 'bin', split_axis=0, concat_axis=0, tiled...]
    reduce_sum x11 -> x0, other arithmetic: 13.4 us -> none  [the longest x6 8.3 us: step(): sq_a = jnp.sum(jnp.square(xblk.astype(jnp.float32)), 1)]
    ppermute x2 -> x0, waiting for transfers between devices: 7.2 us -> none  [from_partner(): return lax.ppermute(value, axis, pairs)]
  transfers between devices with their start and end apart: 6 -> 0, of which waited for: 3 -> 0; matrix products, arithmetic and copies ran while one was open for 22% -> 0% of each run, Pallas kernels for 0% -> 0%
where the time goes in v1:
time: 84.8 us; the launch traced here: 84.6 us
  Pallas kernels  79 us (93%)
  local copies, waits for them, and re-layouts  3.78 us (4%)
  between operations  1.84 us (2%)
    pallas_call x1, Pallas kernels, local(): pl.pallas_call(functools.partial(return_kernel, bins, reps, cap), out_sha...  35.6 us
    pallas_call x1, Pallas kernels, local(): pl.pallas_call(functools.partial(pair_kernel, bins, cap, br, bc), out_sha...  22.9 us
    pallas_call x1, Pallas kernels, local(): pl.pallas_call(functools.partial(scatter_kernel, bins, cap), out_shape=(b...  20.5 us
    unnamed x8, local copies, waits for them, and re-layouts  3.09 us

profile of v1, /device:TPU:1, one launch (start us, length us, event | category | flops | bytes accessed | tf_op | source)
XLA Modules:
  0.0 84.6 jit_solution(1028215639078407186)
XLA Ops:
  0.6 0.7 reshape.9.ids_ref
  1.3 0.0 copy-start
  1.3 1.0 %copy-done = bf16[768,256]{1,0:T(8,128)(2,1)S(1)} copy-done((bf16[768,256]{1,0:T(8,128)(2,1)S(1)}, bf16[768,256]{1,0:T(8,128)(2,1)}, u32[]{:S(2)}) %copy-start) | copy-done | bytes 393240
  2.3 0.0 copy-start.1
  2.3 20.5 %scatter.1 = (bf16[32,48,256]{2,1,0:T(8,128)(2,1)S(1)}, bf16[32,48,256]{2,1,0:T(8,128)(2,1)S(1)}, s32[32,1,128]{2,1,0:T(1,128)S(1)}) custom-call(bf16[768,256]{1,0:T(8,128)(2,1)S(1)} %copy-done, s32[1,768]{1,0:T(1,128)S(1)} %reshape.9.ids_ref), custom_call_target="tpu_custom_call" | custom-call | tf_op jit(solution)/shard_map/scatter/pallas_call | solution.py:347
  22.8 0.0 copy-start.2
  22.9 0.0 copy-done.1
  22.9 0.6 copy-done.2
  23.5 22.9 %pairs.1 = (bf16[32,48,256]{2,1,0:T(8,128)(2,1)S(1)}, f32[2,264,128]{2,1,0:T(8,128)S(1)}) custom-call(s32[32,1,128]{2,1,0:T(1,128)S(1)} %get-tuple-element.11.cnt_ref, f32[3]{0:T(128)S(1)} %copy-done.2, bf16[256,256]{1,0:T(8,128)(2,1)S(1)} %copy-done.1, bf16[32,48,256]{2,1,0:T(8,128)(2,1)S(1)} %get-tuple-element.12.mine_ref, ...), custom_call_target="tpu_custom_call" | custom-call | tf_op jit(solution)/shard_map/pairs/pallas_call | solution.py:361
  46.4 35.6 %giveback.1 = (bf16[768,256]{1,0:T(8,128)(2,1)S(1)}, f32[256,256]{1,0:T(8,128)S(1)}, f32[1,128]{1,0:T(1,128)S(1)}) custom-call(bf16[32,48,256]{2,1,0:T(8,128)(2,1)S(1)} %get-tuple-element.14.slots, f32[2,264,128]{2,1,0:T(8,128)S(1)} %get-tuple-element.15.w_ref, s32[1,768]{1,0:T(1,128)S(1)} %reshape.9.ids_ref), custom_call_target="tpu_custom_call" | custom-call | tf_op jit(solution)/shard_map/giveback/pallas_call | solution.py:378
  82.0 0.7 copy.10
  82.8 0.7 copy.11
Async XLA Ops:
  1.3 1.0 %copy-start = (bf16[768,256]{1,0:T(8,128)(2,1)S(1)}, bf16[768,256]{1,0:T(8,128)(2,1)}, u32[]{:S(2)}) copy-start(bf16[768,256]{1,0:T(8,128)(2,1)} %emb_ref.1) | copy-start | bytes 1179652
  2.3 20.5 %copy-start.1 = (bf16[256,256]{1,0:T(8,128)(2,1)S(1)}, bf16[256,256]{1,0:T(8,128)(2,1)}, u32[]{:S(2)}) copy-start(bf16[256,256]{1,0:T(8,128)(2,1)} %proj_ref.1) | copy-start | bytes 393220
  22.8 0.7 copy-start.2

commit v2 on v1

v2 whole, which is shorter than its diff:
```python
import functools
import math

import jax
import jax.numpy as jnp
from jax import lax
from jax.experimental import pallas as pl
from jax.experimental.pallas import tpu as pltpu
from jax.sharding import PartitionSpec as P

MESH = pl.DeviceIdType.MESH
F32 = jnp.float32
BF16 = jnp.bfloat16
FAR = 1e30
STRIDE = 11
NT = (((1,), (1,)), ((), ()))
TN = (((0,), (0,)), ((), ()))


def iota(shape, dim):
    return lax.broadcasted_iota(jnp.int32, shape, dim)


def slot_places(ids, me, bins, cap):
    half = bins // 2
    jets = ids.shape[1]
    owner = jnp.where(ids >= half, 2 * (ids - half) + 1, 2 * ids)
    step = 256 if jets % 256 == 0 else jets
    before = jnp.where(iota((step, step), 0) < iota((step, step), 1), 1.0, 0.0).astype(BF16)
    wide = max(bins, 16)
    carry = jnp.zeros((wide, 1), F32)
    ranks = []
    for start in range(0, jets, step):
        hot = jnp.where(owner[:, start:start + step] == iota((wide, step), 0), 1.0, 0.0)
        seen = jnp.dot(hot.astype(BF16), before, preferred_element_type=F32) + carry
        ranks.append(jnp.sum(seen * hot, 0, keepdims=True))
        carry = carry + jnp.sum(hot, 1, keepdims=True)
    rank = jnp.concatenate(ranks, 1).astype(jnp.int32)
    away = owner - me
    away = jnp.where(away < 0, away + bins, away)
    turn = lax.rem(away * pow(STRIDE, -1, bins), bins)
    return owner, turn * cap + rank


def line_of(ids_ref):
    return jnp.concatenate([ids_ref[r:r + 1, :] for r in range(ids_ref.shape[0])], 1)


def scatter_kernel(bins, cap, emb_hbm, ids_ref, inbox, pinbox, counts, outbox, mine, emb_ref,
                   cnt_send, cnt_recv, send, recv, fwd_send, fwd_recv, loc):
    z, me = lax.axis_index("dp"), lax.axis_index("bin")
    sib = me + 1 - 2 * lax.rem(me, 2)
    jets = emb_hbm.shape[0]
    fetch = pltpu.make_async_copy(emb_hbm, emb_ref, loc.at[0])
    fetch.start()
    barrier = pltpu.get_barrier_semaphore()
    for k in range(1, bins):
        pl.semaphore_signal(barrier, inc=1, device_id=(z, lax.rem(me + k, bins)), device_id_type=MESH)
    owner, place = slot_places(line_of(ids_ref), me, bins, cap)
    hot = jnp.where(owner == iota((128, jets), 0), 1.0, 0.0).astype(BF16)
    tally = lax.dot_general(jnp.ones((8, jets), BF16), hot, NT, preferred_element_type=F32)
    mine[...] = tally[0:1, :].astype(jnp.int32)
    counts[me] = tally[0:1, :].astype(jnp.int32)
    pl.semaphore_wait(barrier, bins - 1)

    def count_copy(k):
        return pltpu.make_async_remote_copy(
            src_ref=mine, dst_ref=counts.at[me], send_sem=cnt_send.at[k], recv_sem=cnt_recv.at[k],
            device_id=(z, lax.rem(me + STRIDE * k, bins)), device_id_type=MESH)

    def row_copy(k):
        return pltpu.make_async_remote_copy(
            src_ref=outbox.at[k], dst_ref=inbox.at[me], send_sem=send.at[k], recv_sem=recv.at[k],
            device_id=(z, lax.rem(me + STRIDE * k, bins)), device_id_type=MESH)

    for k in range(1, bins):
        count_copy(k).start()
    group = 8 if bins % 8 == 0 else bins
    fetch.wait()
    emb = emb_ref[...]
    for first in range(0, bins, group):
        rows = group * cap
        pick = jnp.where(iota((rows, jets), 0) + first * cap == place, 1.0, 0.0).astype(BF16)
        block = jnp.dot(pick, emb, preferred_element_type=F32).astype(BF16)
        outbox[first:first + group] = block.reshape(group, cap, block.shape[1])
        for k in range(first, first + group):
            if k:
                row_copy(k).start()
    own = pltpu.make_async_copy(outbox.at[0], inbox.at[me], loc.at[1])
    own.start()

    def forward(src):
        return pltpu.make_async_remote_copy(
            src_ref=inbox.at[src], dst_ref=pinbox.at[src], send_sem=fwd_send, recv_sem=fwd_recv,
            device_id=(z, sib), device_id_type=MESH)

    own.wait()
    forward(me).start()
    for k in range(1, bins):
        row_copy(k).wait_recv()
        forward(lax.rem(me + STRIDE * (bins - k), bins)).start()
    for k in range(1, bins):
        count_copy(k).wait()
        row_copy(k).wait_send()
    pltpu.make_async_remote_copy(
        src_ref=inbox, dst_ref=pinbox, send_sem=fwd_send, recv_sem=fwd_recv,
        device_id=(z, sib), device_id_type=MESH).wait()


def pair_kernel(bins, cap, big, cnt_ref, spread_hbm, proj_ref, mine_ref, other_ref, out_ref, w_ref,
                spread_ref, loc, xs, ys, gs, fx, fy, sax, srx, sry, inner, gram, acc, rsum, tot):
    me = lax.axis_index("bin")
    width = proj_ref.shape[0]
    hw = width // 2
    sub = big // 2
    fetch = pltpu.make_async_copy(spread_hbm, spread_ref, loc)
    fetch.start()
    sib = me + 1 - 2 * lax.rem(me, 2)

    def pack(src_ref, dst, column):
        off = 0
        for s in range(bins):
            rows = src_ref[s].astype(F32)
            dst[0, pl.ds(off, cap), :] = rows[:, :hw]
            dst[1, pl.ds(off, cap), :] = rows[:, hw:]
            off = off + cnt_ref[s, 0, column]
        return off

    n_own = pack(mine_ref, xs, me)
    n_oth = pack(other_ref, ys, sib)
    for h in range(2):
        xs[h, pl.ds(n_own, big), :] = jnp.zeros((big, hw), F32)
    proj = proj_ref[...]
    ones = jnp.ones((8, width), BF16)
    subs_own = (n_own + sub - 1) // sub
    subs = (jnp.maximum(n_own, n_oth) + sub - 1) // sub

    def features(rows_ref, feat, col_sq, row_sq, n):
        def body(i, carry):
            base = pl.multiple_of(i * sub, sub)
            emb = jnp.concatenate([rows_ref[0, pl.ds(base, sub), :], rows_ref[1, pl.ds(base, sub), :]], 1)
            emb = jnp.where(iota((sub, width), 0) + base < n, emb, 0.0).astype(BF16)
            val = jnp.dot(emb, proj, preferred_element_type=F32).astype(BF16)
            feat[pl.ds(base, sub), :] = val
            sq = jnp.square(val.astype(F32))
            high = sq.astype(BF16)
            low = (sq - high.astype(F32)).astype(BF16)
            line = lax.dot_general(ones, high, NT, preferred_element_type=F32)
            line = line + lax.dot_general(ones, low, NT, preferred_element_type=F32)
            row_sq[i] = jnp.where(iota((8, sub), 1) + base < n, line, FAR)
            if col_sq is not None:
                col = jnp.broadcast_to(jnp.sum(sq, 1, keepdims=True), (sub, 128))
                col_sq[pl.ds(base, sub), :] = jnp.where(iota((sub, 128), 0) + base < n, col, FAR)
            return carry
        lax.fori_loop(0, subs, body, 0)

    features(xs, fx, sax, srx, n_own)
    features(ys, fy, None, sry, n_oth)

    fetch.wait()
    coef = [1.0 / jnp.full((8, 128), spread_ref[s], F32) / width for s in range(3)]
    rate = [c * math.log2(math.e) for c in coef]
    na = jnp.full((1, 128), jnp.maximum(n_own, 1).astype(F32), F32)
    nc = jnp.full((1, 128), jnp.maximum(n_oth, 1).astype(F32), F32)
    scale = float(bins * cap // 2 * width)
    k_self = jnp.concatenate([scale * (-(4.0 / (na * na)))] * 2, 1)
    k_cross = jnp.concatenate([scale * (4.0 / (na * nc))] * 2, 1)

    tot[...] = jnp.zeros_like(tot)
    w_ref[...] = jnp.zeros_like(w_ref)

    feats = (fx, fy)
    row_sqs = (srx, sry)

    def meet(which, rows, cols, base, col):
        xa = fx[pl.ds(base, rows), :]
        xb = feats[which][pl.ds(pl.multiple_of(col * sub, sub), cols), :]
        inner[which, 0:rows, 0:cols] = lax.dot_general(xa + xa, xb, NT, preferred_element_type=F32)

    def weigh(which, rows, cols, base, col):
        for p in range(0, cols, 128):
            sb = row_sqs[which][col + p // 128]
            total = jnp.zeros((8, 128), F32)
            for r in range(0, rows, 16):
                parts = []
                for q in (r, r + 8):
                    t = inner[which, q:q + 8, p:p + 128] - sax[pl.ds(base + q, 8), :] - sb
                    e0 = jnp.exp2(t * rate[0])
                    e1 = jnp.exp2(t * rate[1])
                    e2 = jnp.exp2(t * rate[2])
                    total = total + (e0 + e1 + e2)
                    parts.append(e0 * coef[0] + e1 * coef[1] + e2 * coef[2])
                gram[which, r:r + 16, p:p + 128] = jnp.concatenate(parts, 0).astype(BF16)
            tot[which] += total

    def pull(which, rows, cols, col):
        xb = feats[which][pl.ds(pl.multiple_of(col * sub, sub), cols), :]
        g = gram[which, 0:rows, 0:cols]
        acc[which, 0:rows, :] += jnp.dot(g, xb, preferred_element_type=F32)
        rsum[which, 0:rows, :] += jnp.dot(g, jnp.ones((cols, 128), BF16), preferred_element_type=F32)

    def row_block(rows, base):
        acc[:, 0:rows, :] = jnp.zeros((2, rows, width), F32)
        rsum[:, 0:rows, :] = jnp.zeros((2, rows, 128), F32)
        blocks = subs // 2

        @pl.when(blocks > 0)
        def _():
            gram[1, 0:rows, :] = jnp.zeros((rows, big), BF16)
            meet(0, rows, big, base, 0)

            def body(j, carry):
                meet(1, rows, big, base, 2 * j)
                pull(1, rows, big, 2 * jnp.maximum(j - 1, 0))
                weigh(0, rows, big, base, 2 * j)
                meet(0, rows, big, base, 2 * jnp.minimum(j + 1, blocks - 1))
                pull(0, rows, big, 2 * j)
                weigh(1, rows, big, base, 2 * j)
                return carry
            lax.fori_loop(0, blocks, body, 0)
            pull(1, rows, big, 2 * (blocks - 1))

        @pl.when(subs % 2 == 1)
        def _():
            for which in (0, 1):
                meet(which, rows, sub, base, subs - 1)
            for which in (0, 1):
                weigh(which, rows, sub, base, subs - 1)
                pull(which, rows, sub, subs - 1)

        xf = fx[pl.ds(base, rows), :].astype(F32)
        force = [xf * jnp.concatenate([rsum[which, 0:rows, :]] * 2, 1) - acc[which, 0:rows, :] for which in (0, 1)]
        gz = (k_self * force[0] + k_cross * force[1]).astype(BF16)
        ge = lax.dot_general(gz, proj, NT, preferred_element_type=F32)
        gs[0, pl.ds(base, rows), :] = ge[:, :hw]
        gs[1, pl.ds(base, rows), :] = ge[:, hw:]
        emb = jnp.concatenate([xs[0, pl.ds(base, rows), :], xs[1, pl.ds(base, rows), :]], 1).astype(BF16)
        gw = lax.dot_general(emb, gz, TN, preferred_element_type=F32)
        w_ref[0, :width, :] += gw[:, :hw]
        w_ref[1, :width, :] += gw[:, hw:]

    def full(i, carry):
        row_block(big, pl.multiple_of(i * big, big))
        return carry
    lax.fori_loop(0, subs_own // 2, full, 0)

    @pl.when(subs_own % 2 == 1)
    def _():
        row_block(sub, pl.multiple_of((subs_own - 1) * sub, sub))

    for h in range(2):
        gs[h, pl.ds(n_own, cap), :] = jnp.zeros((cap, hw), F32)
    share = jnp.sum(tot[0], 0, keepdims=True) / (na * na) - jnp.sum(tot[1], 0, keepdims=True) / (na * nc)
    for h in range(2):
        w_ref[h, width:width + 8, :] = jnp.broadcast_to(share, (8, 128))
    off = 0
    for s in range(bins):
        out_ref[s, :, :hw] = gs[0, pl.ds(off, cap), :].astype(BF16)
        out_ref[s, :, hw:] = gs[1, pl.ds(off, cap), :].astype(BF16)
        off = off + cnt_ref[s, 0, me]


def return_kernel(bins, reps, cap, slots, w_ref, ids_ref, g_out, w_out, l_out,
                  inbox, pick, p_recv, z_send, z_recv, plane, zg, other,
                  send, recv, psem, zsem, asem, zgsem, fsem, loc):
    z, me = lax.axis_index("dp"), lax.axis_index("bin")
    core = lax.rem(me, 2)
    q = lax.div(me, 2)
    chips = bins // 2
    sib = me + 1 - 2 * core
    jets = g_out.shape[0]
    width = g_out.shape[1]
    zr = width // reps
    barrier = pltpu.get_barrier_semaphore()
    for k in range(1, bins):
        pl.semaphore_signal(barrier, inc=1, device_id=(z, lax.rem(me + k, bins)), device_id_type=MESH)
    for k in range(1, reps):
        pl.semaphore_signal(barrier, inc=1, device_id=(lax.rem(z + k, reps), me), device_id_type=MESH)
    pl.semaphore_wait(barrier, bins - 1 + reps - 1)

    def remote(src, dst, ssem, rsem, dev):
        return pltpu.make_async_remote_copy(
            src_ref=src, dst_ref=dst, send_sem=ssem, recv_sem=rsem, device_id=dev, device_id_type=MESH)

    pair = remote(w_ref.at[1 - core], p_recv, psem.at[0], psem.at[1], (z, sib))
    pair.start()

    def row_copy(k):
        dest = lax.rem(me + STRIDE * k, bins)
        return remote(slots.at[dest], inbox.at[bins - k], send, recv, (z, dest))

    for k in range(1, bins):
        row_copy(k).start()
    own = pltpu.make_async_copy(slots.at[me], inbox.at[0], loc)
    own.start()

    _, place = slot_places(line_of(ids_ref), me, bins, cap)

    pair.wait()
    loss_tile = w_ref[core, width:width + 8, :] + p_recv[width:width + 8, :]
    for k in range(reps):
        z_send[k, 0:zr, :] = w_ref[core, k * zr:(k + 1) * zr, :] + p_recv[k * zr:(k + 1) * zr, :]
        z_send[k, zr:zr + 8, :] = loss_tile

    def z_copy(k):
        dest = lax.rem(z + k, reps)
        return remote(z_send.at[dest], z_recv.at[z], zsem.at[0, k], zsem.at[1, k], (dest, me))

    for k in range(1, reps):
        z_copy(k).start()
    z_recv[z] = z_send[z]

    for first in range(0, jets, 128 if jets % 128 == 0 else jets):
        size = min(128, jets - first)
        part = jnp.broadcast_to(place[:, first:first + size], (size, size))
        column = jnp.sum(jnp.where(iota((size, size), 0) == iota((size, size), 1), part, 0), 1, keepdims=True)
        pick[first:first + size, :] = jnp.where(column == iota((size, bins * cap), 1), 1.0, 0.0).astype(BF16)

    for k in range(1, reps):
        z_copy(k).wait()
    chunk = z_recv[0]
    for k in range(1, reps):
        chunk = chunk + z_recv[k]
    plane[q] = chunk

    def plane_copy(k):
        dest = lax.rem(q + k, chips)
        return remote(plane.at[q], plane.at[q], asem.at[0, k], asem.at[1, k], (z, 2 * dest + core))

    for k in range(1, chips):
        plane_copy(k).start()

    own.wait()
    remote(slots.at[pl.ds(0, bins - 1)], inbox.at[pl.ds(1, bins - 1)], send, recv, (z, sib)).wait()
    g_out[...] = jnp.dot(pick[...], inbox[...].reshape(bins * cap, width), preferred_element_type=F32).astype(BF16)

    for k in range(1, chips):
        plane_copy(k).wait()
    whole = plane[0]
    for k in range(1, chips):
        whole = whole + plane[k]
    l_out[...] = jnp.broadcast_to(jnp.sum(whole[zr:zr + 1, :], 1, keepdims=True) / reps, (1, 128))
    zg[z] = whole[0:zr, :]

    def zg_copy(k):
        dest = lax.rem(z + k, reps)
        return remote(zg.at[z], zg.at[z], zgsem.at[0, k], zgsem.at[1, k], (dest, me))

    def hand_over(at):
        return remote(zg.at[at], other.at[at], fsem.at[0], fsem.at[1], (z, sib))

    for k in range(1, reps):
        zg_copy(k).start()
    hand_over(z).start()
    for k in range(1, reps):
        zg_copy(k).wait_recv()
        hand_over(lax.rem(z + reps - k, reps)).start()
    for k in range(1, reps):
        zg_copy(k).wait_send()
    remote(zg, other, fsem.at[0], fsem.at[1], (z, sib)).wait()
    tokens = float(jets * bins * reps)
    here = zg[...].reshape(width, 128) / tokens
    there = other[...].reshape(width, 128) / tokens
    w_out[:, 0:128] = jnp.where(core == 0, here, there)
    w_out[:, 128:256] = jnp.where(core == 0, there, here)


def vmem(count):
    return [pl.BlockSpec(memory_space=pltpu.VMEM)] * count


def local(embeddings, bin_ids, spreads, projection):
    jets, width = embeddings.shape
    bins, reps = lax.axis_size("bin"), lax.axis_size("dp")
    cap = 2 * jets // bins
    most = bins * cap
    chips = bins // 2
    ids = bin_ids.reshape(-1, 128) if jets % 128 == 0 else bin_ids.reshape(1, jets)
    dma = pltpu.SemaphoreType.DMA
    box = jax.ShapeDtypeStruct((bins, cap, width), BF16)
    limit = 48 << 20
    inbox, pinbox, counts = pl.pallas_call(
        functools.partial(scatter_kernel, bins, cap),
        out_shape=(box, box, jax.ShapeDtypeStruct((bins, 1, 128), jnp.int32)),
        in_specs=[pl.BlockSpec(memory_space=pltpu.HBM)] + vmem(1), out_specs=tuple(vmem(3)),
        scratch_shapes=[
            pltpu.VMEM((bins, cap, width), BF16), pltpu.VMEM((1, 128), jnp.int32), pltpu.VMEM((jets, width), BF16),
            dma((bins,)), dma((bins,)), dma((bins,)), dma((bins,)), dma, dma, dma((2,))],
        compiler_params=pltpu.CompilerParams(collective_id=0, has_side_effects=True, vmem_limit_bytes=limit),
        name="scatter",
    )(embeddings, ids)

    big = 256
    top = -(-most // big) * big
    room = top + big
    slots, w_part = pl.pallas_call(
        functools.partial(pair_kernel, bins, cap, big),
        out_shape=(box, jax.ShapeDtypeStruct((2, width + 8, 128), F32)),
        in_specs=[pl.BlockSpec(memory_space=pltpu.SMEM), pl.BlockSpec(memory_space=pltpu.HBM)] + vmem(3),
        out_specs=tuple(vmem(2)),
        scratch_shapes=[
            pltpu.SMEM((3,), F32), dma,
            pltpu.VMEM((2, room, width // 2), F32), pltpu.VMEM((2, room, width // 2), F32),
            pltpu.VMEM((2, room, width // 2), F32),
            pltpu.VMEM((top, width), BF16), pltpu.VMEM((top, width), BF16), pltpu.VMEM((top, 128), F32),
            pltpu.VMEM((2 * top // big, 8, big // 2), F32), pltpu.VMEM((2 * top // big, 8, big // 2), F32),
            pltpu.VMEM((2, big, big), F32), pltpu.VMEM((2, big, big), BF16),
            pltpu.VMEM((2, big, width), F32), pltpu.VMEM((2, big, 128), F32), pltpu.VMEM((2, 8, 128), F32)],
        compiler_params=pltpu.CompilerParams(vmem_limit_bytes=limit),
        name="pairs",
    )(counts, spreads, projection, inbox, pinbox)

    zr = width // reps
    grad_emb, grad_w, loss = pl.pallas_call(
        functools.partial(return_kernel, bins, reps, cap),
        out_shape=(jax.ShapeDtypeStruct((jets, width), BF16), jax.ShapeDtypeStruct((width, width), F32),
                   jax.ShapeDtypeStruct((1, 128), F32)),
        in_specs=vmem(3), out_specs=tuple(vmem(3)),
        scratch_shapes=[
            pltpu.VMEM((bins, cap, width), BF16), pltpu.VMEM((jets, most), BF16),
            pltpu.VMEM((width + 8, 128), F32),
            pltpu.VMEM((reps, zr + 8, 128), F32), pltpu.VMEM((reps, zr + 8, 128), F32),
            pltpu.VMEM((chips, zr + 8, 128), F32), pltpu.VMEM((reps, zr, 128), F32), pltpu.VMEM((reps, zr, 128), F32),
            dma, dma, dma((2,)), dma((2, reps)), dma((2, chips)), dma((2, reps)), dma((2,)), dma],
        compiler_params=pltpu.CompilerParams(collective_id=1, has_side_effects=True, vmem_limit_bytes=limit),
        name="giveback",
    )(slots, w_part, ids)
    return grad_emb, grad_w, loss[0, 0]


def solution(mesh):
    return jax.shard_map(
        local,
        mesh=mesh,
        in_specs=(P(("dp", "bin"), None), P(("dp", "bin")), P(), P()),
        out_specs=(P(("dp", "bin"), None), P(), P()),
        check_vma=False,
    )
```

time: 84.8 us -> 74.9 us (0.88)
  Pallas kernels: 79 us -> 69.1 us
    pallas_call x1, Pallas kernels: 22.9 us -> 15.1 us  [local(): pl.pallas_call(functools.partial(pair_kernel, bins, cap, big), out_shape=...]
    pallas_call x1, Pallas kernels: 35.6 us -> 32.7 us  [local(): pl.pallas_call(functools.partial(return_kernel, bins, reps, cap), out_sha...]
    unnamed x8 -> x10, local copies, waits for them, and re-layouts: 3.09 us -> 3.77 us
where the time goes in v2:
time: 74.9 us; the launch traced here: 74.7 us
  Pallas kernels  69.1 us (92%)
  local copies, waits for them, and re-layouts  3.77 us (5%)
  between operations  1.85 us (2%)
    pallas_call x1, Pallas kernels, local(): pl.pallas_call(functools.partial(return_kernel, bins, reps, cap), out_sha...  32.7 us
    pallas_call x1, Pallas kernels, local(): pl.pallas_call(functools.partial(scatter_kernel, bins, cap), out_shape=(b...  21.3 us
    pallas_call x1, Pallas kernels, local(): pl.pallas_call(functools.partial(pair_kernel, bins, cap, big), out_shape=...  15.1 us
    unnamed x10, local copies, waits for them, and re-layouts  3.77 us

profile of v2, /device:TPU:1, one launch (start us, length us, event | category | flops | bytes accessed | tf_op | source)
XLA Modules:
  0.0 74.7 jit_solution(12926243761267444071)
XLA Ops:
  0.6 0.0 copy-start
  0.6 1.0 %copy-done = bf16[768,256]{1,0:T(8,128)(2,1)S(1)} copy-done((bf16[768,256]{1,0:T(8,128)(2,1)S(1)}, bf16[768,256]{1,0:T(8,128)(2,1)}, u32[]{:S(2)}) %copy-start) | copy-done | bytes 393240
  1.6 0.0 copy-start.2
  1.6 0.7 copy-done.2
  2.3 0.0 copy-start.1
  2.3 21.3 %scatter.1 = (bf16[32,48,256]{2,1,0:T(8,128)(2,1)S(1)}, bf16[32,48,256]{2,1,0:T(8,128)(2,1)S(1)}, s32[32,1,128]{2,1,0:T(1,128)S(1)}) custom-call(bf16[768,256]{1,0:T(8,128)(2,1)S(1)} %copy-done, s32[6,128]{1,0:T(8,128)S(1)} %bitcast.3), custom_call_target="tpu_custom_call" | custom-call | tf_op jit(solution)/shard_map/scatter/pallas_call | solution.py:382
  23.6 0.0 copy-start.3
  23.6 0.0 copy-done.1
  23.6 0.6 copy-done.3
  24.3 15.1 %pairs.1 = (bf16[32,48,256]{2,1,0:T(8,128)(2,1)S(1)}, f32[2,264,128]{2,1,0:T(8,128)S(1)}) custom-call(s32[32,1,128]{2,1,0:T(1,128)S(1)} %get-tuple-element.11.cnt_ref, f32[3]{0:T(128)S(1)} %copy-done.3, bf16[256,256]{1,0:T(8,128)(2,1)S(1)} %copy-done.1, bf16[32,48,256]{2,1,0:T(8,128)(2,1)S(1)} %get-tuple-element.12.mine_ref, ...), custom_call_target="tpu_custom_call" | custom-call | tf_op jit(solution)/shard_map/pairs/pallas_call | solution.py:396
  39.4 32.7 %giveback.1 = (bf16[768,256]{1,0:T(8,128)(2,1)S(1)}, f32[256,256]{1,0:T(8,128)S(1)}, f32[1,128]{1,0:T(1,128)S(1)}) custom-call(bf16[32,48,256]{2,1,0:T(8,128)(2,1)S(1)} %get-tuple-element.14.slots, f32[2,264,128]{2,1,0:T(8,128)S(1)} %get-tuple-element.15.w_ref, s32[6,128]{1,0:T(8,128)S(1)} %bitcast.4), custom_call_target="tpu_custom_call" | custom-call | tf_op jit(solution)/shard_map/giveback/pallas_call | solution.py:414
  72.1 0.7 %copy.10 = bf16[768,256]{1,0:T(8,128)(2,1)} copy(bf16[768,256]{1,0:T(8,128)(2,1)S(1)} %get-tuple-element.22) | data formatting | bytes 786432
  72.9 0.7 copy.11
Async XLA Ops:
  0.6 1.0 %copy-start = (bf16[768,256]{1,0:T(8,128)(2,1)S(1)}, bf16[768,256]{1,0:T(8,128)(2,1)}, u32[]{:S(2)}) copy-start(bf16[768,256]{1,0:T(8,128)(2,1)} %emb_hbm.1) | copy-start | bytes 1179652
  1.6 0.7 copy-start.2
  2.3 21.3 %copy-start.1 = (bf16[256,256]{1,0:T(8,128)(2,1)S(1)}, bf16[256,256]{1,0:T(8,128)(2,1)}, u32[]{:S(2)}) copy-start(bf16[256,256]{1,0:T(8,128)(2,1)} %proj_ref.1) | copy-start | bytes 393220
  23.6 0.7 copy-start.3

commit v3 on v2

v3 whole, which is shorter than its diff:
```python
import functools
import math

import jax
import jax.numpy as jnp
from jax import lax
from jax.experimental import pallas as pl
from jax.experimental.pallas import tpu as pltpu
from jax.sharding import PartitionSpec as P

MESH = pl.DeviceIdType.MESH
F32 = jnp.float32
BF16 = jnp.bfloat16
FAR = 1e30
EMPTY = 1024.0
NT = (((1,), (1,)), ((), ()))
TN = (((0,), (0,)), ((), ()))


def iota(shape, dim):
    return lax.broadcasted_iota(jnp.int32, shape, dim)


def grid_of(bins):
    chips = bins // 2
    nx = max(d for d in range(1, chips + 1) if chips % d == 0 and d * d <= chips)
    return nx, chips // nx


def hops(step, size):
    return min(step, size - step)


def plane_steps(bins):
    nx, ny = grid_of(bins)
    steps = [(dx, dy) for dx in range(nx) for dy in range(ny)]
    return sorted(steps, key=lambda d: -(hops(d[0], nx) + hops(d[1], ny)))


def turns(bins):
    ny = grid_of(bins)[1]
    codes = [2 * (dx * ny + dy) + dc for dx, dy in plane_steps(bins) for dc in range(2)]
    return [code for code in codes if code]


def back(code, bins):
    nx, ny = grid_of(bins)
    dx, dy, dc = code // (2 * ny), code // 2 % ny, code % 2
    return 2 * ((-dx % nx) * ny + -dy % ny) + dc


def chip_at(q, dx, dy, bins):
    nx, ny = grid_of(bins)
    return lax.rem(lax.div(q, ny) + dx, nx) * ny + lax.rem(lax.rem(q, ny) + dy, ny)


def device_at(me, code, bins):
    ny = grid_of(bins)[1]
    chip = chip_at(lax.div(me, 2), code // (2 * ny), code // 2 % ny, bins)
    return 2 * chip + lax.rem(lax.rem(me, 2) + code % 2, 2)


def slot_places(ids, me, bins, cap):
    nx, ny = grid_of(bins)
    half = bins // 2
    jets = ids.shape[1]
    upper = ids >= half
    chip = jnp.where(upper, ids - half, ids)
    dx = chip // ny - lax.div(me, 2 * ny)
    dx = jnp.where(dx < 0, dx + nx, dx)
    dy = chip % ny - lax.rem(lax.div(me, 2), ny)
    dy = jnp.where(dy < 0, dy + ny, dy)
    dc = jnp.where(upper, 1, 0) - lax.rem(me, 2)
    code = 2 * (dx * ny + dy) + jnp.where(dc < 0, 1, dc)
    step = 256 if jets % 256 == 0 else jets
    before = jnp.where(iota((step, step), 0) < iota((step, step), 1), 1.0, 0.0).astype(BF16)
    wide = max(bins, 16)
    carry = jnp.zeros((wide, 1), F32)
    ranks = []
    for start in range(0, jets, step):
        hot = jnp.where(code[:, start:start + step] == iota((wide, step), 0), 1.0, 0.0)
        seen = jnp.dot(hot.astype(BF16), before, preferred_element_type=F32) + carry
        ranks.append(jnp.sum(seen * hot, 0, keepdims=True))
        carry = carry + jnp.sum(hot, 1, keepdims=True)
    rank = jnp.concatenate(ranks, 1).astype(jnp.int32)
    return code * cap + rank


def line_of(ids_ref):
    return jnp.concatenate([ids_ref[r:r + 1, :] for r in range(ids_ref.shape[0])], 1)


def scatter_kernel(bins, cap, emb_hbm, ids_hbm, inbox, pinbox, counts, pcounts, outbox, emb_ref, ids_ref,
                   send, recv, fwd_send, fwd_recv, cnt_sem, loc):
    z, me = lax.axis_index("dp"), lax.axis_index("bin")
    sib = me + 1 - 2 * lax.rem(me, 2)
    jets = emb_hbm.shape[0]
    fetch_ids = pltpu.make_async_copy(ids_hbm, ids_ref, loc.at[1])
    fetch_ids.start()
    fetch = pltpu.make_async_copy(emb_hbm, emb_ref, loc.at[0])
    fetch.start()
    barrier = pltpu.get_barrier_semaphore()
    for k in range(1, bins):
        pl.semaphore_signal(barrier, inc=1, device_id=(z, lax.rem(me + k, bins)), device_id_type=MESH)
    fetch_ids.wait()
    place = slot_places(line_of(ids_ref), me, bins, cap)

    def row_copy(k):
        return pltpu.make_async_remote_copy(
            src_ref=outbox.at[k], dst_ref=inbox.at[me], send_sem=send, recv_sem=recv.at[k],
            device_id=(z, device_at(me, k, bins)), device_id_type=MESH)

    group = 8 if bins % 8 == 0 else bins
    fetch.wait()
    emb = emb_ref[...]
    solid = jnp.ones((jets, 128), BF16)
    for first in range(0, bins, group):
        rows = group * cap
        pick = jnp.where(iota((rows, jets), 0) + first * cap == place, 1.0, 0.0).astype(BF16)
        block = jnp.dot(pick, emb, preferred_element_type=F32)
        taken = jnp.dot(pick, solid, preferred_element_type=F32)
        outbox[first:first + group, :, 0:128] = jnp.where(
            taken > 0.5, block[:, 0:128], EMPTY).astype(BF16).reshape(group, cap, 128)
        outbox[first:first + group, :, 128:256] = block[:, 128:256].astype(BF16).reshape(group, cap, 128)
    pl.semaphore_wait(barrier, bins - 1)
    for k in turns(bins):
        row_copy(k).start()
    own = pltpu.make_async_copy(outbox.at[0], inbox.at[me], loc.at[1])
    own.start()

    def forward(src):
        return pltpu.make_async_remote_copy(
            src_ref=inbox.at[src], dst_ref=pinbox.at[src], send_sem=fwd_send, recv_sem=fwd_recv,
            device_id=(z, sib), device_id_type=MESH)

    def tally(src):
        live = jnp.where(inbox[src, :, 0:128].astype(F32) < EMPTY / 2, 1.0, 0.0)
        return jnp.where(iota((1, 128), 1) == src, jnp.sum(live, 0, keepdims=True), 0.0)

    own.wait()
    forward(me).start()
    table = tally(me)
    for k in turns(bins):
        row_copy(k).wait_recv()
        src = device_at(me, back(k, bins), bins)
        forward(src).start()
        table = table + tally(src)
    counts[...] = table.astype(jnp.int32)
    swap = pltpu.make_async_remote_copy(
        src_ref=counts, dst_ref=pcounts, send_sem=cnt_sem.at[0], recv_sem=cnt_sem.at[1],
        device_id=(z, sib), device_id_type=MESH)
    swap.start()
    pltpu.make_async_remote_copy(
        src_ref=outbox.at[pl.ds(1, bins - 1)], dst_ref=inbox.at[pl.ds(1, bins - 1)], send_sem=send, recv_sem=fwd_recv,
        device_id=(z, sib), device_id_type=MESH).wait_send()
    swap.wait()
    pltpu.make_async_remote_copy(
        src_ref=inbox, dst_ref=pinbox, send_sem=fwd_send, recv_sem=fwd_recv,
        device_id=(z, sib), device_id_type=MESH).wait()


def pair_kernel(bins, cap, big, cnt_ref, pcnt_ref, spread_hbm, proj_ref, mine_ref, other_ref, out_ref, w_ref,
                spread_ref, loc, xs, ys, gs, fx, fy, sax, srx, sry, inner, gram, acc, rsum, tot):
    width = proj_ref.shape[0]
    hw = width // 2
    sub = big // 2
    fetch = pltpu.make_async_copy(spread_hbm, spread_ref, loc)
    fetch.start()

    def pack(src_ref, dst, cnt):
        off = 0
        for s in range(bins):
            rows = src_ref[s].astype(F32)
            dst[0, pl.ds(off, cap), :] = rows[:, :hw]
            dst[1, pl.ds(off, cap), :] = rows[:, hw:]
            off = off + cnt[0, s]
        return off

    n_own = pack(mine_ref, xs, cnt_ref)
    n_oth = pack(other_ref, ys, pcnt_ref)
    for h in range(2):
        xs[h, pl.ds(n_own, big), :] = jnp.zeros((big, hw), F32)
    proj = proj_ref[...]
    ones = jnp.ones((8, width), BF16)
    subs_own = (n_own + sub - 1) // sub
    subs = (jnp.maximum(n_own, n_oth) + sub - 1) // sub

    def features(i, carry):
        base = pl.multiple_of(i * big, big)
        for rows_ref, feat, col_sq, row_sq, n in ((xs, fx, sax, srx, n_own), (ys, fy, None, sry, n_oth)):
            emb = jnp.concatenate([rows_ref[0, pl.ds(base, big), :], rows_ref[1, pl.ds(base, big), :]], 1)
            emb = jnp.where(iota((big, width), 0) + base < n, emb, 0.0).astype(BF16)
            val = jnp.dot(emb, proj, preferred_element_type=F32).astype(BF16)
            feat[pl.ds(base, big), :] = val
            sq = jnp.square(val.astype(F32))
            high = sq.astype(BF16)
            low = (sq - high.astype(F32)).astype(BF16)
            line = lax.dot_general(ones, high, NT, preferred_element_type=F32)
            line = line + lax.dot_general(ones, low, NT, preferred_element_type=F32)
            line = jnp.where(iota((8, big), 1) + base < n, line, FAR)
            row_sq[2 * i] = line[:, 0:sub]
            row_sq[2 * i + 1] = line[:, sub:big]
            if col_sq is not None:
                col = jnp.broadcast_to(jnp.sum(sq, 1, keepdims=True), (big, 128))
                col_sq[pl.ds(base, big), :] = jnp.where(iota((big, 128), 0) + base < n, col, FAR)
        return carry
    lax.fori_loop(0, (subs + 1) // 2, features, 0)

    fetch.wait()
    coef = [1.0 / jnp.full((8, 128), spread_ref[s], F32) / width for s in range(3)]
    rate = [c * math.log2(math.e) for c in coef]
    na = jnp.full((1, 128), jnp.maximum(n_own, 1).astype(F32), F32)
    nc = jnp.full((1, 128), jnp.maximum(n_oth, 1).astype(F32), F32)
    scale = float(bins * cap // 2 * width)
    k_self = jnp.concatenate([scale * (-(4.0 / (na * na)))] * 2, 1)
    k_cross = jnp.concatenate([scale * (4.0 / (na * nc))] * 2, 1)

    tot[...] = jnp.zeros_like(tot)
    w_ref[...] = jnp.zeros_like(w_ref)

    feats = (fx, fy)
    row_sqs = (srx, sry)

    def meet(which, rows, cols, base, col, at=0):
        xa = fx[pl.ds(base, rows), :]
        xb = feats[which][pl.ds(pl.multiple_of(col * sub, sub) + at, cols), :]
        inner[which, 0:rows, at:at + cols] = lax.dot_general(xa + xa, xb, NT, preferred_element_type=F32)

    def weigh(which, rows, cols, base, col, beside=()):
        steps = [(p, r) for p in range(0, cols, 128) for r in range(0, rows, 16)]
        beside = list(beside)
        every = max(1, len(steps) // (len(beside) + 1))
        total = jnp.zeros((8, 128), F32)
        for at, (p, r) in enumerate(steps):
            if beside and at % every == 0:
                beside.pop(0)()
            sb = row_sqs[which][col + p // sub, :, p % sub:p % sub + 128]
            parts = []
            for q in (r, r + 8):
                t = inner[which, q:q + 8, p:p + 128] - sax[pl.ds(base + q, 8), :] - sb
                e0 = jnp.exp2(t * rate[0])
                e1 = jnp.exp2(t * rate[1])
                e2 = jnp.exp2(t * rate[2])
                total = total + (e0 + e1 + e2)
                parts.append(e0 * coef[0] + e1 * coef[1] + e2 * coef[2])
            gram[which, r:r + 16, p:p + 128] = jnp.concatenate(parts, 0).astype(BF16)
        tot[which] += total
        for rest in beside:
            rest()

    def pull(which, rows, cols, col):
        xb = feats[which][pl.ds(pl.multiple_of(col * sub, sub), cols), :]
        acc[which, 0:rows, :] += jnp.dot(gram[which, 0:rows, 0:cols], xb, preferred_element_type=F32)

    def count(which, rows, cols):
        rsum[which, 0:rows, :] += jnp.dot(
            gram[which, 0:rows, 0:cols], jnp.ones((cols, 128), BF16), preferred_element_type=F32)

    def row_block(rows, base):
        acc[:, 0:rows, :] = jnp.zeros((2, rows, width), F32)
        rsum[:, 0:rows, :] = jnp.zeros((2, rows, 128), F32)
        blocks = subs // 2

        @pl.when(blocks > 0)
        def _():
            gram[1, 0:rows, :] = jnp.zeros((rows, big), BF16)
            meet(0, rows, big, base, 0)

            def turn(which, j, prev, later):
                other = 1 - which
                weigh(which, rows, big, base, 2 * j, [
                    lambda: meet(other, rows, sub, base, later, 0),
                    lambda: meet(other, rows, sub, base, later, sub),
                    lambda: pull(other, rows, big, prev),
                    lambda: count(other, rows, big)])

            def body(j, carry):
                turn(0, j, 2 * jnp.maximum(j - 1, 0), 2 * j)
                turn(1, j, 2 * j, 2 * jnp.minimum(j + 1, blocks - 1))
                return carry
            lax.fori_loop(0, blocks, body, 0)
            pull(1, rows, big, 2 * (blocks - 1))
            count(1, rows, big)

        @pl.when(subs % 2 == 1)
        def _():
            for which in (0, 1):
                meet(which, rows, sub, base, subs - 1)
            for which in (0, 1):
                weigh(which, rows, sub, base, subs - 1)
                pull(which, rows, sub, subs - 1)
                count(which, rows, sub)

        xf = fx[pl.ds(base, rows), :].astype(F32)
        force = [xf * jnp.concatenate([rsum[which, 0:rows, :]] * 2, 1) - acc[which, 0:rows, :] for which in (0, 1)]
        gz = (k_self * force[0] + k_cross * force[1]).astype(BF16)
        ge = lax.dot_general(gz, proj, NT, preferred_element_type=F32)
        gs[0, pl.ds(base, rows), :] = ge[:, :hw]
        gs[1, pl.ds(base, rows), :] = ge[:, hw:]
        emb = jnp.concatenate([xs[0, pl.ds(base, rows), :], xs[1, pl.ds(base, rows), :]], 1).astype(BF16)
        gw = lax.dot_general(emb, gz, TN, preferred_element_type=F32)
        w_ref[0, :width, :] += gw[:, :hw]
        w_ref[1, :width, :] += gw[:, hw:]

    def full(i, carry):
        row_block(big, pl.multiple_of(i * big, big))
        return carry
    lax.fori_loop(0, subs_own // 2, full, 0)

    @pl.when(subs_own % 2 == 1)
    def _():
        row_block(sub, pl.multiple_of((subs_own - 1) * sub, sub))

    for h in range(2):
        gs[h, pl.ds(n_own, cap), :] = jnp.zeros((cap, hw), F32)
    share = jnp.sum(tot[0], 0, keepdims=True) / (na * na) - jnp.sum(tot[1], 0, keepdims=True) / (na * nc)
    for h in range(2):
        w_ref[h, width:width + 8, :] = jnp.broadcast_to(share, (8, 128))
    off = 0
    for s in range(bins):
        out_ref[s, :, :hw] = gs[0, pl.ds(off, cap), :].astype(BF16)
        out_ref[s, :, hw:] = gs[1, pl.ds(off, cap), :].astype(BF16)
        off = off + cnt_ref[0, s]


def return_kernel(bins, reps, cap, slots, w_ref, ids_ref, g_out, w_out, l_out,
                  inbox, pick, p_recv, a_send, a_recv, zx, full, other,
                  send, recv, psem, asem, zsem, gsem, fsem, loc):
    z, me = lax.axis_index("dp"), lax.axis_index("bin")
    core = lax.rem(me, 2)
    q = lax.div(me, 2)
    chips = bins // 2
    sib = me + 1 - 2 * core
    jets = g_out.shape[0]
    width = g_out.shape[1]
    ar = width // chips
    tokens = float(jets * bins * reps)
    barrier = pltpu.get_barrier_semaphore()
    for k in range(1, bins):
        pl.semaphore_signal(barrier, inc=1, device_id=(z, lax.rem(me + k, bins)), device_id_type=MESH)
    for k in range(1, reps):
        pl.semaphore_signal(barrier, inc=1, device_id=(lax.rem(z + k, reps), me), device_id_type=MESH)

    place = slot_places(line_of(ids_ref), me, bins, cap)
    for first in range(0, jets, 128 if jets % 128 == 0 else jets):
        size = min(128, jets - first)
        part = jnp.broadcast_to(place[:, first:first + size], (size, size))
        column = jnp.sum(jnp.where(iota((size, size), 0) == iota((size, size), 1), part, 0), 1, keepdims=True)
        pick[first:first + size, :] = jnp.where(column == iota((size, bins * cap), 1), 1.0, 0.0).astype(BF16)
    pl.semaphore_wait(barrier, bins - 1 + reps - 1)

    def remote(src, dst, sems, dev):
        return pltpu.make_async_remote_copy(
            src_ref=src, dst_ref=dst, send_sem=sems.at[0], recv_sem=sems.at[1], device_id=dev, device_id_type=MESH)

    pair = remote(w_ref.at[1 - core], p_recv, psem, (z, sib))
    pair.start()

    def row_copy(k):
        dest = device_at(me, k, bins)
        return pltpu.make_async_remote_copy(
            src_ref=slots.at[dest], dst_ref=inbox.at[back(k, bins)], send_sem=send, recv_sem=recv,
            device_id=(z, dest), device_id_type=MESH)

    own = pltpu.make_async_copy(slots.at[me], inbox.at[0], loc)
    own.start()
    around = sorted(range(1, reps), key=lambda k: -hops(k, reps))

    pair.wait()
    loss_tile = w_ref[core, width:width + 8, :] + p_recv[width:width + 8, :]
    for k in range(chips):
        a_send[k, 0:ar, :] = w_ref[core, k * ar:(k + 1) * ar, :] + p_recv[k * ar:(k + 1) * ar, :]
        a_send[k, ar:ar + 8, :] = loss_tile

    others = [chip_at(q, dx, dy, bins) for dx, dy in plane_steps(bins) if dx or dy]
    for chip in others:
        remote(a_send.at[chip], a_recv.at[q], asem, (z, 2 * chip + core)).start()
    a_recv[q] = a_send[q]
    remote(a_send.at[pl.ds(0, chips - 1)], a_recv.at[pl.ds(0, chips - 1)], asem, (z, sib)).wait()
    for k in turns(bins):
        row_copy(k).start()
    chunk = a_recv[0]
    for k in range(1, chips):
        chunk = chunk + a_recv[k]
    zx[z] = chunk
    for k in around:
        remote(zx.at[z], zx.at[z], zsem, (lax.rem(z + k, reps), me)).start()
    remote(zx.at[pl.ds(0, reps - 1)], zx.at[pl.ds(0, reps - 1)], zsem, (z, sib)).wait()
    chunk = zx[0]
    for k in range(1, reps):
        chunk = chunk + zx[k]
    full[q] = chunk[0:ar, :] / tokens
    for chip in others:
        remote(full.at[q], full.at[q], gsem, (z, 2 * chip + core)).start()
    l_out[...] = jnp.broadcast_to(jnp.sum(chunk[ar:ar + 1, :], 1, keepdims=True) / reps, (1, 128))

    own.wait()
    pltpu.make_async_remote_copy(
        src_ref=slots.at[pl.ds(0, bins - 1)], dst_ref=inbox.at[pl.ds(1, bins - 1)], send_sem=send, recv_sem=recv,
        device_id=(z, sib), device_id_type=MESH).wait()
    g_out[...] = jnp.dot(pick[...], inbox[...].reshape(bins * cap, width), preferred_element_type=F32).astype(BF16)

    remote(full.at[pl.ds(0, chips - 1)], full.at[pl.ds(0, chips - 1)], gsem, (z, sib)).wait()
    last = remote(full, other, fsem, (z, sib))
    last.start()
    last.wait()
    here = full[...].reshape(width, 128)
    there = other[...].reshape(width, 128)
    w_out[:, 0:128] = jnp.where(core == 0, here, there)
    w_out[:, 128:256] = jnp.where(core == 0, there, here)


def vmem(count):
    return [pl.BlockSpec(memory_space=pltpu.VMEM)] * count


def local(embeddings, bin_ids, spreads, projection):
    jets, width = embeddings.shape
    bins, reps = lax.axis_size("bin"), lax.axis_size("dp")
    cap = 2 * jets // bins
    most = bins * cap
    chips = bins // 2
    ids = bin_ids.reshape(-1, 128) if jets % 128 == 0 else bin_ids.reshape(1, jets)
    dma = pltpu.SemaphoreType.DMA
    box = jax.ShapeDtypeStruct((bins, cap, width), BF16)
    limit = 48 << 20
    tally = jax.ShapeDtypeStruct((1, 128), jnp.int32)
    inbox, pinbox, counts, pcounts = pl.pallas_call(
        functools.partial(scatter_kernel, bins, cap),
        out_shape=(box, box, tally, tally),
        in_specs=[pl.BlockSpec(memory_space=pltpu.HBM)] * 2, out_specs=tuple(vmem(4)),
        scratch_shapes=[
            pltpu.VMEM((bins, cap, width), BF16), pltpu.VMEM((jets, width), BF16), pltpu.VMEM(ids.shape, jnp.int32),
            dma, dma((bins,)), dma, dma, dma((2,)), dma((2,))],
        compiler_params=pltpu.CompilerParams(collective_id=0, has_side_effects=True, vmem_limit_bytes=limit),
        name="scatter",
    )(embeddings, ids)

    big = 512
    top = -(-most // big) * big
    room = top + big
    slots, w_part = pl.pallas_call(
        functools.partial(pair_kernel, bins, cap, big),
        out_shape=(box, jax.ShapeDtypeStruct((2, width + 8, 128), F32)),
        in_specs=[pl.BlockSpec(memory_space=pltpu.SMEM)] * 2 + [pl.BlockSpec(memory_space=pltpu.HBM)] + vmem(3),
        out_specs=tuple(vmem(2)),
        scratch_shapes=[
            pltpu.SMEM((3,), F32), dma,
            pltpu.VMEM((2, room, width // 2), F32), pltpu.VMEM((2, room, width // 2), F32),
            pltpu.VMEM((2, room, width // 2), F32),
            pltpu.VMEM((top, width), BF16), pltpu.VMEM((top, width), BF16), pltpu.VMEM((top, 128), F32),
            pltpu.VMEM((2 * top // big, 8, big // 2), F32), pltpu.VMEM((2 * top // big, 8, big // 2), F32),
            pltpu.VMEM((2, big, big), F32), pltpu.VMEM((2, big, big), BF16),
            pltpu.VMEM((2, big, width), F32), pltpu.VMEM((2, big, 128), F32), pltpu.VMEM((2, 8, 128), F32)],
        compiler_params=pltpu.CompilerParams(vmem_limit_bytes=limit),
        name="pairs",
    )(counts, pcounts, spreads, projection, inbox, pinbox)

    ar = width // chips
    grad_emb, grad_w, loss = pl.pallas_call(
        functools.partial(return_kernel, bins, reps, cap),
        out_shape=(jax.ShapeDtypeStruct((jets, width), BF16), jax.ShapeDtypeStruct((width, width), F32),
                   jax.ShapeDtypeStruct((1, 128), F32)),
        in_specs=vmem(3), out_specs=tuple(vmem(3)),
        scratch_shapes=[
            pltpu.VMEM((bins, cap, width), BF16), pltpu.VMEM((jets, most), BF16),
            pltpu.VMEM((width + 8, 128), F32),
            pltpu.VMEM((chips, ar + 8, 128), F32), pltpu.VMEM((chips, ar + 8, 128), F32),
            pltpu.VMEM((reps, ar + 8, 128), F32), pltpu.VMEM((chips, ar, 128), F32), pltpu.VMEM((chips, ar, 128), F32),
            dma, dma, dma((2,)), dma((2,)), dma((2,)), dma((2,)), dma((2,)), dma],
        compiler_params=pltpu.CompilerParams(collective_id=1, has_side_effects=True, vmem_limit_bytes=limit),
        name="giveback",
    )(slots, w_part, ids)
    return grad_emb, grad_w, loss[0, 0]


def solution(mesh):
    return jax.shard_map(
        local,
        mesh=mesh,
        in_specs=(P(("dp", "bin"), None), P(("dp", "bin")), P(), P()),
        out_specs=(P(("dp", "bin"), None), P(), P()),
        check_vma=False,
    )
```

time: 74.9 us -> 65.7 us (0.88)
  Pallas kernels: 69.1 us -> 59.9 us
    pallas_call x1, Pallas kernels: 32.7 us -> 28 us  [local(): pl.pallas_call(functools.partial(return_kernel, bins, reps, cap), out_sha...]
    pallas_call x1, Pallas kernels: 15.1 us -> 12.8 us  [local(): pl.pallas_call(functools.partial(pair_kernel, bins, cap, big), out_shape=...]
    pallas_call x1, Pallas kernels: 21.3 us -> 19.1 us  [local(): pl.pallas_call(functools.partial(scatter_kernel, bins, cap), out_shape=(b...]
where the time goes in v3:
time: 65.7 us; the launch traced here: 65.5 us
  Pallas kernels  59.9 us (91%)
  local copies, waits for them, and re-layouts  3.77 us (6%)
  between operations  1.85 us (3%)
    pallas_call x1, Pallas kernels, local(): pl.pallas_call(functools.partial(return_kernel, bins, reps, cap), out_sha...  28 us
    pallas_call x1, Pallas kernels, local(): pl.pallas_call(functools.partial(scatter_kernel, bins, cap), out_shape=(b...  19.1 us
    pallas_call x1, Pallas kernels, local(): pl.pallas_call(functools.partial(pair_kernel, bins, cap, big), out_shape=...  12.8 us
    unnamed x10, local copies, waits for them, and re-layouts  3.77 us

profile of v3, /device:TPU:1, one launch (start us, length us, event | category | flops | bytes accessed | tf_op | source)
XLA Modules:
  0.0 65.5 jit_solution(16153263040223260040)
XLA Ops:
  0.6 0.0 copy-start
  0.6 1.0 %copy-done = bf16[768,256]{1,0:T(8,128)(2,1)S(1)} copy-done((bf16[768,256]{1,0:T(8,128)(2,1)S(1)}, bf16[768,256]{1,0:T(8,128)(2,1)}, u32[]{:S(2)}) %copy-start) | copy-done | bytes 393240
  1.6 0.0 copy-start.2
  1.6 0.7 %copy-done.2 = s32[768]{0:T(1024)S(1)} copy-done((s32[768]{0:T(1024)S(1)}, s32[768]{0:T(1024)}, u32[]{:S(2)}) %copy-start.2) | copy-done | bytes 3096
  2.3 0.0 copy-start.1
  2.3 19.1 %scatter.1 = (bf16[32,48,256]{2,1,0:T(8,128)(2,1)S(1)}, bf16[32,48,256]{2,1,0:T(8,128)(2,1)S(1)}, s32[1,128]{1,0:T(1,128)S(1)}, s32[1,128]{1,0:T(1,128)S(1)}) custom-call(bf16[768,256]{1,0:T(8,128)(2,1)S(1)} %copy-done, s32[6,128]{1,0:T(8,128)S(1)} %bitcast.3), custom_call_target="tpu_custom_call" | custom-call | tf_op jit(solution)/shard_map/scatter/pallas_call | solution.py:428
  21.4 0.0 copy-start.3
  21.4 0.0 copy-done.1
  21.4 0.6 copy-done.3
  22.1 12.8 %pairs.1 = (bf16[32,48,256]{2,1,0:T(8,128)(2,1)S(1)}, f32[2,264,128]{2,1,0:T(8,128)S(1)}) custom-call(s32[1,128]{1,0:T(1,128)S(1)} %get-tuple-element.12.cnt_ref, s32[1,128]{1,0:T(1,128)S(1)} %get-tuple-element.13.pcnt_ref, f32[3]{0:T(128)S(1)} %copy-done.3, bf16[256,256]{1,0:T(8,128)(2,1)S(1)} %copy-done.1, ...), custom_call_target="tpu_custom_call" | custom-call | tf_op jit(solution)/shard_map/pairs/pallas_call | solution.py:442
  34.9 28.0 %giveback.1 = (bf16[768,256]{1,0:T(8,128)(2,1)S(1)}, f32[256,256]{1,0:T(8,128)S(1)}, f32[1,128]{1,0:T(1,128)S(1)}) custom-call(bf16[32,48,256]{2,1,0:T(8,128)(2,1)S(1)} %get-tuple-element.16.slots, f32[2,264,128]{2,1,0:T(8,128)S(1)} %get-tuple-element.17.w_ref, s32[6,128]{1,0:T(8,128)S(1)} %bitcast.4), custom_call_target="tpu_custom_call" | custom-call | tf_op jit(solution)/shard_map/giveback/pallas_call | solution.py:460
  62.9 0.7 %copy.10 = bf16[768,256]{1,0:T(8,128)(2,1)} copy(bf16[768,256]{1,0:T(8,128)(2,1)S(1)} %get-tuple-element.24) | data formatting | bytes 786432
  63.6 0.7 %copy.11 = f32[256,256]{1,0:T(8,128)} copy(f32[256,256]{1,0:T(8,128)S(1)} %get-tuple-element.25) | data formatting | bytes 524288
Async XLA Ops:
  0.6 1.0 %copy-start = (bf16[768,256]{1,0:T(8,128)(2,1)S(1)}, bf16[768,256]{1,0:T(8,128)(2,1)}, u32[]{:S(2)}) copy-start(bf16[768,256]{1,0:T(8,128)(2,1)} %emb_hbm.1) | copy-start | bytes 1179652
  1.6 0.7 %copy-start.2 = (s32[768]{0:T(1024)S(1)}, s32[768]{0:T(1024)}, u32[]{:S(2)}) copy-start(s32[768]{0:T(1024)} %param.5) | copy-start | bytes 9220
  2.3 19.1 %copy-start.1 = (bf16[256,256]{1,0:T(8,128)(2,1)S(1)}, bf16[256,256]{1,0:T(8,128)(2,1)}, u32[]{:S(2)}) copy-start(bf16[256,256]{1,0:T(8,128)(2,1)} %proj_ref.1) | copy-start | bytes 393220
  21.4 0.7 %copy-start.3 = (f32[3]{0:T(128)S(1)}, f32[3]{0:T(128)}, u32[]{:S(2)}) copy-start(f32[3]{0:T(128)} %spread_hbm.1) | copy-start | bytes 40

commit v4 on v3

--- a/solution.py
+++ b/solution.py
@@ -376,8 +376,10 @@
     for chip in others:
         remote(a_send.at[chip], a_recv.at[q], asem, (z, 2 * chip + core)).start()
     a_recv[q] = a_send[q]
+    for k in turns(bins)[0:8]:
+        row_copy(k).start()
     remote(a_send.at[pl.ds(0, chips - 1)], a_recv.at[pl.ds(0, chips - 1)], asem, (z, sib)).wait()
-    for k in turns(bins):
+    for k in turns(bins)[8:24]:
         row_copy(k).start()
     chunk = a_recv[0]
     for k in range(1, chips):
@@ -392,17 +394,19 @@
     full[q] = chunk[0:ar, :] / tokens
     for chip in others:
         remote(full.at[q], full.at[q], gsem, (z, 2 * chip + core)).start()
+    for k in turns(bins)[24:31]:
+        row_copy(k).start()
     l_out[...] = jnp.broadcast_to(jnp.sum(chunk[ar:ar + 1, :], 1, keepdims=True) / reps, (1, 128))
 
+    remote(full.at[pl.ds(0, chips - 1)], full.at[pl.ds(0, chips - 1)], gsem, (z, sib)).wait()
+    last = remote(full, other, fsem, (z, sib))
+    last.start()
     own.wait()
     pltpu.make_async_remote_copy(
         src_ref=slots.at[pl.ds(0, bins - 1)], dst_ref=inbox.at[pl.ds(1, bins - 1)], send_sem=send, recv_sem=recv,
         device_id=(z, sib), device_id_type=MESH).wait()
     g_out[...] = jnp.dot(pick[...], inbox[...].reshape(bins * cap, width), preferred_element_type=F32).astype(BF16)
 
-    remote(full.at[pl.ds(0, chips - 1)], full.at[pl.ds(0, chips - 1)], gsem, (z, sib)).wait()
-    last = remote(full, other, fsem, (z, sib))
-    last.start()
     last.wait()
     here = full[...].reshape(width, 128)
     there = other[...].reshape(width, 128)

time: 65.7 us -> 63.2 us (0.962)
  Pallas kernels: 59.9 us -> 57.4 us
    pallas_call x1, Pallas kernels: 28 us -> 25.5 us  [local(): pl.pallas_call(functools.partial(return_kernel, bins, reps, cap), out_sha...]
where the time goes in v4:
time: 63.2 us; the launch traced here: 63 us
  Pallas kernels  57.4 us (91%)
  local copies, waits for them, and re-layouts  3.77 us (6%)
  between operations  1.85 us (3%)
    pallas_call x1, Pallas kernels, local(): pl.pallas_call(functools.partial(return_kernel, bins, reps, cap), out_sha...  25.5 us
    pallas_call x1, Pallas kernels, local(): pl.pallas_call(functools.partial(scatter_kernel, bins, cap), out_shape=(b...  19.1 us
    pallas_call x1, Pallas kernels, local(): pl.pallas_call(functools.partial(pair_kernel, bins, cap, big), out_shape=...  12.8 us
    unnamed x10, local copies, waits for them, and re-layouts  3.77 us

profile of v4, /device:TPU:1, one launch (start us, length us, event | category | flops | bytes accessed | tf_op | source)
XLA Modules:
  0.0 63.0 jit_solution(10262935252948092738)
XLA Ops:
  0.6 0.0 copy-start
  0.6 1.0 %copy-done = bf16[768,256]{1,0:T(8,128)(2,1)S(1)} copy-done((bf16[768,256]{1,0:T(8,128)(2,1)S(1)}, bf16[768,256]{1,0:T(8,128)(2,1)}, u32[]{:S(2)}) %copy-start) | copy-done | bytes 393240
  1.6 0.0 copy-start.2
  1.6 0.7 %copy-done.2 = s32[768]{0:T(1024)S(1)} copy-done((s32[768]{0:T(1024)S(1)}, s32[768]{0:T(1024)}, u32[]{:S(2)}) %copy-start.2) | copy-done | bytes 3096
  2.3 0.0 copy-start.1
  2.3 19.1 %scatter.1 = (bf16[32,48,256]{2,1,0:T(8,128)(2,1)S(1)}, bf16[32,48,256]{2,1,0:T(8,128)(2,1)S(1)}, s32[1,128]{1,0:T(1,128)S(1)}, s32[1,128]{1,0:T(1,128)S(1)}) custom-call(bf16[768,256]{1,0:T(8,128)(2,1)S(1)} %copy-done, s32[6,128]{1,0:T(8,128)S(1)} %bitcast.3), custom_call_target="tpu_custom_call" | custom-call | tf_op jit(solution)/shard_map/scatter/pallas_call | solution.py:432
  21.4 0.0 copy-start.3
  21.4 0.0 copy-done.1
  21.4 0.6 %copy-done.3 = f32[3]{0:T(128)S(1)} copy-done((f32[3]{0:T(128)S(1)}, f32[3]{0:T(128)}, u32[]{:S(2)}) %copy-start.3) | copy-done | bytes 36
  22.1 12.8 %pairs.1 = (bf16[32,48,256]{2,1,0:T(8,128)(2,1)S(1)}, f32[2,264,128]{2,1,0:T(8,128)S(1)}) custom-call(s32[1,128]{1,0:T(1,128)S(1)} %get-tuple-element.12.cnt_ref, s32[1,128]{1,0:T(1,128)S(1)} %get-tuple-element.13.pcnt_ref, f32[3]{0:T(128)S(1)} %copy-done.3, bf16[256,256]{1,0:T(8,128)(2,1)S(1)} %copy-done.1, ...), custom_call_target="tpu_custom_call" | custom-call | tf_op jit(solution)/shard_map/pairs/pallas_call | solution.py:446
  34.9 25.5 %giveback.1 = (bf16[768,256]{1,0:T(8,128)(2,1)S(1)}, f32[256,256]{1,0:T(8,128)S(1)}, f32[1,128]{1,0:T(1,128)S(1)}) custom-call(bf16[32,48,256]{2,1,0:T(8,128)(2,1)S(1)} %get-tuple-element.16.slots, f32[2,264,128]{2,1,0:T(8,128)S(1)} %get-tuple-element.17.w_ref, s32[6,128]{1,0:T(8,128)S(1)} %bitcast.4), custom_call_target="tpu_custom_call" | custom-call | tf_op jit(solution)/shard_map/giveback/pallas_call | solution.py:464
  60.4 0.7 %copy.10 = bf16[768,256]{1,0:T(8,128)(2,1)} copy(bf16[768,256]{1,0:T(8,128)(2,1)S(1)} %get-tuple-element.24) | data formatting | bytes 786432
  61.2 0.7 %copy.11 = f32[256,256]{1,0:T(8,128)} copy(f32[256,256]{1,0:T(8,128)S(1)} %get-tuple-element.25) | data formatting | bytes 524288
Async XLA Ops:
  0.6 1.0 %copy-start = (bf16[768,256]{1,0:T(8,128)(2,1)S(1)}, bf16[768,256]{1,0:T(8,128)(2,1)}, u32[]{:S(2)}) copy-start(bf16[768,256]{1,0:T(8,128)(2,1)} %emb_hbm.1) | copy-start | bytes 1179652
  1.6 0.7 %copy-start.2 = (s32[768]{0:T(1024)S(1)}, s32[768]{0:T(1024)}, u32[]{:S(2)}) copy-start(s32[768]{0:T(1024)} %param.5) | copy-start | bytes 9220
  2.3 19.1 %copy-start.1 = (bf16[256,256]{1,0:T(8,128)(2,1)S(1)}, bf16[256,256]{1,0:T(8,128)(2,1)}, u32[]{:S(2)}) copy-start(bf16[256,256]{1,0:T(8,128)(2,1)} %proj_ref.1) | copy-start | bytes 393220
  21.4 0.7 %copy-start.3 = (f32[3]{0:T(128)S(1)}, f32[3]{0:T(128)}, u32[]{:S(2)}) copy-start(f32[3]{0:T(128)} %spread_hbm.1) | copy-start | bytes 40

commit v5 on v4

--- a/solution.py
+++ b/solution.py
@@ -367,10 +367,10 @@
     around = sorted(range(1, reps), key=lambda k: -hops(k, reps))
 
     pair.wait()
-    loss_tile = w_ref[core, width:width + 8, :] + p_recv[width:width + 8, :]
+    loss_tile = w_ref[core, width:width + 1, :] + p_recv[width:width + 1, :]
     for k in range(chips):
         a_send[k, 0:ar, :] = w_ref[core, k * ar:(k + 1) * ar, :] + p_recv[k * ar:(k + 1) * ar, :]
-        a_send[k, ar:ar + 8, :] = loss_tile
+        a_send[k, ar:ar + 1, :] = loss_tile
 
     others = [chip_at(q, dx, dy, bins) for dx, dy in plane_steps(bins) if dx or dy]
     for chip in others:
@@ -469,8 +469,8 @@
         scratch_shapes=[
             pltpu.VMEM((bins, cap, width), BF16), pltpu.VMEM((jets, most), BF16),
             pltpu.VMEM((width + 8, 128), F32),
-            pltpu.VMEM((chips, ar + 8, 128), F32), pltpu.VMEM((chips, ar + 8, 128), F32),
-            pltpu.VMEM((reps, ar + 8, 128), F32), pltpu.VMEM((chips, ar, 128), F32), pltpu.VMEM((chips, ar, 128), F32),
+            pltpu.VMEM((chips, ar + 1, 128), F32), pltpu.VMEM((chips, ar + 1, 128), F32),
+            pltpu.VMEM((reps, ar + 1, 128), F32), pltpu.VMEM((chips, ar, 128), F32), pltpu.VMEM((chips, ar, 128), F32),
             dma, dma, dma((2,)), dma((2,)), dma((2,)), dma((2,)), dma((2,)), dma],
         compiler_params=pltpu.CompilerParams(collective_id=1, has_side_effects=True, vmem_limit_bytes=limit),
         name="giveback",

time: 63.2 us -> 63.5 us (level)
  no operation moved by 1% of the time
where the time goes in v5:
time: 63.5 us; the launch traced here: 63.3 us
  Pallas kernels  57.7 us (91%)
  local copies, waits for them, and re-layouts  3.77 us (6%)
  between operations  1.85 us (3%)
    pallas_call x1, Pallas kernels, local(): pl.pallas_call(functools.partial(return_kernel, bins, reps, cap), out_sha...  25.8 us
    pallas_call x1, Pallas kernels, local(): pl.pallas_call(functools.partial(scatter_kernel, bins, cap), out_shape=(b...  19.1 us
    pallas_call x1, Pallas kernels, local(): pl.pallas_call(functools.partial(pair_kernel, bins, cap, big), out_shape=...  12.8 us
    unnamed x10, local copies, waits for them, and re-layouts  3.77 us

profile of v5, /device:TPU:1, one launch (start us, length us, event | category | flops | bytes accessed | tf_op | source)
XLA Modules:
  0.0 63.3 jit_solution(1814594172261439147)
XLA Ops:
  0.6 0.0 copy-start
  0.6 1.0 %copy-done = bf16[768,256]{1,0:T(8,128)(2,1)S(1)} copy-done((bf16[768,256]{1,0:T(8,128)(2,1)S(1)}, bf16[768,256]{1,0:T(8,128)(2,1)}, u32[]{:S(2)}) %copy-start) | copy-done | bytes 393240
  1.6 0.0 copy-start.2
  1.6 0.7 %copy-done.2 = s32[768]{0:T(1024)S(1)} copy-done((s32[768]{0:T(1024)S(1)}, s32[768]{0:T(1024)}, u32[]{:S(2)}) %copy-start.2) | copy-done | bytes 3096
  2.3 0.0 copy-start.1
  2.3 19.1 %scatter.1 = (bf16[32,48,256]{2,1,0:T(8,128)(2,1)S(1)}, bf16[32,48,256]{2,1,0:T(8,128)(2,1)S(1)}, s32[1,128]{1,0:T(1,128)S(1)}, s32[1,128]{1,0:T(1,128)S(1)}) custom-call(bf16[768,256]{1,0:T(8,128)(2,1)S(1)} %copy-done, s32[6,128]{1,0:T(8,128)S(1)} %bitcast.3), custom_call_target="tpu_custom_call" | custom-call | tf_op jit(solution)/shard_map/scatter/pallas_call | solution.py:432
  21.4 0.0 copy-start.3
  21.4 0.0 copy-done.1
  21.4 0.6 %copy-done.3 = f32[3]{0:T(128)S(1)} copy-done((f32[3]{0:T(128)S(1)}, f32[3]{0:T(128)}, u32[]{:S(2)}) %copy-start.3) | copy-done | bytes 36
  22.1 12.8 %pairs.1 = (bf16[32,48,256]{2,1,0:T(8,128)(2,1)S(1)}, f32[2,264,128]{2,1,0:T(8,128)S(1)}) custom-call(s32[1,128]{1,0:T(1,128)S(1)} %get-tuple-element.12.cnt_ref, s32[1,128]{1,0:T(1,128)S(1)} %get-tuple-element.13.pcnt_ref, f32[3]{0:T(128)S(1)} %copy-done.3, bf16[256,256]{1,0:T(8,128)(2,1)S(1)} %copy-done.1, ...), custom_call_target="tpu_custom_call" | custom-call | tf_op jit(solution)/shard_map/pairs/pallas_call | solution.py:446
  34.9 25.8 %giveback.1 = (bf16[768,256]{1,0:T(8,128)(2,1)S(1)}, f32[256,256]{1,0:T(8,128)S(1)}, f32[1,128]{1,0:T(1,128)S(1)}) custom-call(bf16[32,48,256]{2,1,0:T(8,128)(2,1)S(1)} %get-tuple-element.16.slots, f32[2,264,128]{2,1,0:T(8,128)S(1)} %get-tuple-element.17.w_ref, s32[6,128]{1,0:T(8,128)S(1)} %bitcast.4), custom_call_target="tpu_custom_call" | custom-call | tf_op jit(solution)/shard_map/giveback/pallas_call | solution.py:464
  60.7 0.7 %copy.10 = bf16[768,256]{1,0:T(8,128)(2,1)} copy(bf16[768,256]{1,0:T(8,128)(2,1)S(1)} %get-tuple-element.24) | data formatting | bytes 786432
  61.4 0.7 %copy.11 = f32[256,256]{1,0:T(8,128)} copy(f32[256,256]{1,0:T(8,128)S(1)} %get-tuple-element.25) | data formatting | bytes 524288
Async XLA Ops:
  0.6 1.0 %copy-start = (bf16[768,256]{1,0:T(8,128)(2,1)S(1)}, bf16[768,256]{1,0:T(8,128)(2,1)}, u32[]{:S(2)}) copy-start(bf16[768,256]{1,0:T(8,128)(2,1)} %emb_hbm.1) | copy-start | bytes 1179652
  1.6 0.7 %copy-start.2 = (s32[768]{0:T(1024)S(1)}, s32[768]{0:T(1024)}, u32[]{:S(2)}) copy-start(s32[768]{0:T(1024)} %param.5) | copy-start | bytes 9220
  2.3 19.1 %copy-start.1 = (bf16[256,256]{1,0:T(8,128)(2,1)S(1)}, bf16[256,256]{1,0:T(8,128)(2,1)}, u32[]{:S(2)}) copy-start(bf16[256,256]{1,0:T(8,128)(2,1)} %proj_ref.1) | copy-start | bytes 393220
  21.4 0.7 %copy-start.3 = (f32[3]{0:T(128)S(1)}, f32[3]{0:T(128)}, u32[]{:S(2)}) copy-start(f32[3]{0:T(128)} %spread_hbm.1) | copy-start | bytes 40

commit v6 on v5

--- a/solution.py
+++ b/solution.py
@@ -90,19 +90,14 @@
     return jnp.concatenate([ids_ref[r:r + 1, :] for r in range(ids_ref.shape[0])], 1)
 
 
-def scatter_kernel(bins, cap, emb_hbm, ids_hbm, inbox, pinbox, counts, pcounts, outbox, emb_ref, ids_ref,
+def scatter_kernel(bins, cap, emb_ref, ids_ref, inbox, pinbox, counts, pcounts, outbox,
                    send, recv, fwd_send, fwd_recv, cnt_sem, loc):
     z, me = lax.axis_index("dp"), lax.axis_index("bin")
     sib = me + 1 - 2 * lax.rem(me, 2)
-    jets = emb_hbm.shape[0]
-    fetch_ids = pltpu.make_async_copy(ids_hbm, ids_ref, loc.at[1])
-    fetch_ids.start()
-    fetch = pltpu.make_async_copy(emb_hbm, emb_ref, loc.at[0])
-    fetch.start()
+    jets = emb_ref.shape[0]
     barrier = pltpu.get_barrier_semaphore()
     for k in range(1, bins):
         pl.semaphore_signal(barrier, inc=1, device_id=(z, lax.rem(me + k, bins)), device_id_type=MESH)
-    fetch_ids.wait()
     place = slot_places(line_of(ids_ref), me, bins, cap)
 
     def row_copy(k):
@@ -111,7 +106,6 @@
             device_id=(z, device_at(me, k, bins)), device_id_type=MESH)
 
     group = 8 if bins % 8 == 0 else bins
-    fetch.wait()
     emb = emb_ref[...]
     solid = jnp.ones((jets, 128), BF16)
     for first in range(0, bins, group):
@@ -125,7 +119,7 @@
     pl.semaphore_wait(barrier, bins - 1)
     for k in turns(bins):
         row_copy(k).start()
-    own = pltpu.make_async_copy(outbox.at[0], inbox.at[me], loc.at[1])
+    own = pltpu.make_async_copy(outbox.at[0], inbox.at[me], loc)
     own.start()
 
     def forward(src):
@@ -432,10 +426,10 @@
     inbox, pinbox, counts, pcounts = pl.pallas_call(
         functools.partial(scatter_kernel, bins, cap),
         out_shape=(box, box, tally, tally),
-        in_specs=[pl.BlockSpec(memory_space=pltpu.HBM)] * 2, out_specs=tuple(vmem(4)),
+        in_specs=vmem(2), out_specs=tuple(vmem(4)),
         scratch_shapes=[
-            pltpu.VMEM((bins, cap, width), BF16), pltpu.VMEM((jets, width), BF16), pltpu.VMEM(ids.shape, jnp.int32),
-            dma, dma((bins,)), dma, dma, dma((2,)), dma((2,))],
+            pltpu.VMEM((bins, cap, width), BF16),
+            dma, dma((bins,)), dma, dma, dma((2,)), dma],
         compiler_params=pltpu.CompilerParams(collective_id=0, has_side_effects=True, vmem_limit_bytes=limit),
         name="scatter",
     )(embeddings, ids)

time: 63.5 us -> 62.2 us (0.980)
  Pallas kernels: 57.7 us -> 56 us
    pallas_call x1, Pallas kernels: 25.8 us -> 24.6 us  [local(): pl.pallas_call(functools.partial(return_kernel, bins, reps, cap), out_sha...]
where the time goes in v6:
time: 62.2 us; the launch traced here: 61.6 us
  Pallas kernels  56 us (90%)
  local copies, waits for them, and re-layouts  3.77 us (6%)
  between operations  1.85 us (3%)
    pallas_call x1, Pallas kernels, local(): pl.pallas_call(functools.partial(return_kernel, bins, reps, cap), out_sha...  24.6 us
    pallas_call x1, Pallas kernels, local(): pl.pallas_call(functools.partial(scatter_kernel, bins, cap), out_shape=(b...  18.8 us
    pallas_call x1, Pallas kernels, local(): pl.pallas_call(functools.partial(pair_kernel, bins, cap, big), out_shape=...  12.6 us
    unnamed x10, local copies, waits for them, and re-layouts  3.77 us

profile of v6, /device:TPU:1, one launch (start us, length us, event | category | flops | bytes accessed | tf_op | source)
XLA Modules:
  0.0 61.6 jit_solution(7549005608143087023)
XLA Ops:
  0.6 0.0 copy-start
  0.6 1.0 %copy-done = bf16[768,256]{1,0:T(8,128)(2,1)S(1)} copy-done((bf16[768,256]{1,0:T(8,128)(2,1)S(1)}, bf16[768,256]{1,0:T(8,128)(2,1)}, u32[]{:S(2)}) %copy-start) | copy-done | bytes 393240
  1.6 0.0 copy-start.2
  1.6 0.7 %copy-done.2 = s32[768]{0:T(1024)S(1)} copy-done((s32[768]{0:T(1024)S(1)}, s32[768]{0:T(1024)}, u32[]{:S(2)}) %copy-start.2) | copy-done | bytes 3096
  2.3 0.0 copy-start.1
  2.3 18.8 %scatter.1 = (bf16[32,48,256]{2,1,0:T(8,128)(2,1)S(1)}, bf16[32,48,256]{2,1,0:T(8,128)(2,1)S(1)}, s32[1,128]{1,0:T(1,128)S(1)}, s32[1,128]{1,0:T(1,128)S(1)}) custom-call(bf16[768,256]{1,0:T(8,128)(2,1)S(1)} %copy-done, s32[6,128]{1,0:T(8,128)S(1)} %bitcast.3), custom_call_target="tpu_custom_call" | custom-call | tf_op jit(solution)/shard_map/scatter/pallas_call | solution.py:426
  21.1 0.0 copy-start.3
  21.1 0.0 copy-done.1
  21.1 0.6 %copy-done.3 = f32[3]{0:T(128)S(1)} copy-done((f32[3]{0:T(128)S(1)}, f32[3]{0:T(128)}, u32[]{:S(2)}) %copy-start.3) | copy-done | bytes 36
  21.8 12.6 %pairs.1 = (bf16[32,48,256]{2,1,0:T(8,128)(2,1)S(1)}, f32[2,264,128]{2,1,0:T(8,128)S(1)}) custom-call(s32[1,128]{1,0:T(1,128)S(1)} %get-tuple-element.12.cnt_ref, s32[1,128]{1,0:T(1,128)S(1)} %get-tuple-element.13.pcnt_ref, f32[3]{0:T(128)S(1)} %copy-done.3, bf16[256,256]{1,0:T(8,128)(2,1)S(1)} %copy-done.1, ...), custom_call_target="tpu_custom_call" | custom-call | tf_op jit(solution)/shard_map/pairs/pallas_call | solution.py:440
  34.4 24.6 %giveback.1 = (bf16[768,256]{1,0:T(8,128)(2,1)S(1)}, f32[256,256]{1,0:T(8,128)S(1)}, f32[1,128]{1,0:T(1,128)S(1)}) custom-call(bf16[32,48,256]{2,1,0:T(8,128)(2,1)S(1)} %get-tuple-element.16.slots, f32[2,264,128]{2,1,0:T(8,128)S(1)} %get-tuple-element.17.w_ref, s32[6,128]{1,0:T(8,128)S(1)} %bitcast.4), custom_call_target="tpu_custom_call" | custom-call | tf_op jit(solution)/shard_map/giveback/pallas_call | solution.py:458
  59.0 0.7 %copy.10 = bf16[768,256]{1,0:T(8,128)(2,1)} copy(bf16[768,256]{1,0:T(8,128)(2,1)S(1)} %get-tuple-element.24) | data formatting | bytes 786432
  59.7 0.7 %copy.11 = f32[256,256]{1,0:T(8,128)} copy(f32[256,256]{1,0:T(8,128)S(1)} %get-tuple-element.25) | data formatting | bytes 524288
Async XLA Ops:
  0.6 1.0 %copy-start = (bf16[768,256]{1,0:T(8,128)(2,1)S(1)}, bf16[768,256]{1,0:T(8,128)(2,1)}, u32[]{:S(2)}) copy-start(bf16[768,256]{1,0:T(8,128)(2,1)} %emb_ref.1) | copy-start | bytes 1179652
  1.6 0.7 %copy-start.2 = (s32[768]{0:T(1024)S(1)}, s32[768]{0:T(1024)}, u32[]{:S(2)}) copy-start(s32[768]{0:T(1024)} %param.5) | copy-start | bytes 9220
  2.3 18.8 %copy-start.1 = (bf16[256,256]{1,0:T(8,128)(2,1)S(1)}, bf16[256,256]{1,0:T(8,128)(2,1)}, u32[]{:S(2)}) copy-start(bf16[256,256]{1,0:T(8,128)(2,1)} %proj_ref.1) | copy-start | bytes 393220
  21.1 0.7 %copy-start.3 = (f32[3]{0:T(128)S(1)}, f32[3]{0:T(128)}, u32[]{:S(2)}) copy-start(f32[3]{0:T(128)} %spread_hbm.1) | copy-start | bytes 40
